TPU v7x, 256 devices: a whole 4x4x8 slice. The times are simulated.
256 devices in a mesh: feat: 8 (over x, core), rows: 32 (over y, z).
Axes of the slice: x: 4, y: 4, z: 8, core: 2. Of those that a mesh axis runs over, the one named last changes fastest.
Arguments:
- samples: float32 [440, 262144], P(None, ('feat', 'rows')), may hold values from -6 to 6, as said below
- residual: float32 [147, 262144], P(None, ('feat', 'rows')), may hold values from -12 to 12, as said below
- bank: float32 [8, 440, 1024], P(None, None, 'feat'), may hold values from -0.25 to 0.25
- bank_phase: float32 [8, 1024], P(None, 'feat'), may hold values from -3.140625 to 3.140625
- bank_weights: float32 [8, 147, 1024], P(None, None, 'feat'), may hold values from -4 to 4
- block_index: int32 [1], replicated, may hold values from 0 to 7
Outputs:
- new_weights: float32 [147, 1024], P(None, 'feat')
- new_residual: float32 [147, 262144], P(None, ('feat', 'rows'))
Inputs may be any that keep to these rules, and one draw needn't show every extreme that they name: `samples`: frames of the input features. `residual`: targets that depend partly on the frames.
All inputs are finite; a program needn't handle non-finite values.
Results may differ from a plain program's by a relative error of at most 0.0003.
Values sent between devices are 32-bit elements; how exact they have to be, the bound alone decides.
No kernel may reach another device: no remote copies, remote signals or barrier semaphores. Data moves between devices by JAX's collectives and lax.ppermute only.
A program may use at most 128 MiB of HBM per device.

v0:
```python
import jax
import jax.numpy as jnp
from jax import lax
from jax.experimental import pallas as pl
from jax.experimental.pallas import tpu as pltpu
from jax.sharding import PartitionSpec as P

ridge_weight = 0.05
D = 440
C = 147
FB = 1024
NB = 8
PAD = 152
COLS = 1024
OFF = [0]
for _k in range(NB):
    OFF.append(OFF[-1] + (NB - _k) * 128 + PAD)
T = OFF[-1]
HALF = T // 2
QUART = T // 8
CHUNK = 24
TURN = 0.15915494309189535
COS = (0.9999999890590223, -19.739204499453898, 64.93911745989527, -85.4501395308797, 60.167630950920234, -25.967599248327534, 6.528658161042403)
f32 = jnp.float32
bf16 = jnp.bfloat16
NN = (((1,), (0,)), ((), ()))
NT = (((1,), (1,)), ((), ()))


def dot(l, r, dims):
    return lax.dot_general(l, r, dims, preferred_element_type=f32)


def split2(x):
    a = x.astype(bf16)
    return a, (x - a.astype(f32)).astype(bf16)


def split3(x):
    a = x.astype(bf16)
    r = x - a.astype(f32)
    b = r.astype(bf16)
    return a, b, (r - b.astype(f32)).astype(bf16)


def gram_kernel(meta, proj, samples, residual, weights, packed, fh, fl):
    s = jnp.concatenate([samples[...], jnp.zeros((8, COLS), f32)], axis=0)
    sh, sl = split2(s)
    for f in range(8):
        turned = (proj[meta[f]] * TURN).T
        h, l = split2(turned)
        y = dot(h, sh, NN) + dot(h, sl, NN) + dot(l, sh, NN) + turned[:, D : D + 1]
        r = y - jnp.round(y)
        z = r * r
        c = jnp.full_like(z, COS[-1])
        for a in COS[-2::-1]:
            c = c * z + a
        ch, cl = split2(c)
        fh[128 * f : 128 * f + 128, :] = ch
        fl[128 * f : 128 * f + 128, :] = cl
    rh, rl = split2(jnp.concatenate([residual[...], jnp.zeros((PAD - C, COLS), f32)], axis=0))
    inv = 1.0 / (COLS * 256)

    def put(at, value):
        n = value.shape[0]
        low = min(max(HALF - at, 0), n)
        if low > 0:
            packed[meta[9], at : at + low, :] = value[:low]
        if low < n:
            packed[1 - meta[9], at + low - HALF : at + n - HALF, :] = value[low:]

    ridge = jnp.concatenate([weights[...], jnp.zeros((PAD - C, 128), f32)], axis=0) * (-ridge_weight)
    for q in range(4):
        o = 256 * q
        ch, cl = fh[o : o + 256, :], fl[o : o + 256, :]
        g = (dot(fh[o:, :], ch, NT) + dot(fh[o:, :], cl, NT) + dot(fl[o:, :], ch, NT)) * inv
        r = (dot(rh, ch, NT) + dot(rh, cl, NT) + dot(rl, ch, NT)) * inv
        for j in range(2):
            k = 2 * q + j
            m = (NB - k) * 128
            put(OFF[k], g[128 * j :, 128 * j : 128 * j + 128])
            own = jnp.where(meta[8] == k, 1.0, 0.0)
            put(OFF[k] + m, r[:, 128 * j : 128 * j + 128] + ridge * own)


def tree(xs):
    xs = list(xs)
    while len(xs) > 1:
        last = [xs[-1]] if len(xs) % 2 else []
        xs = [xs[i] + xs[i + 1] for i in range(0, len(xs) - 1, 2)] + last
    return xs[0]


def sweep_slab(rows, lane, sub):
    d = list(rows)
    n = len(d)
    for g in range(n):
        c0 = 8 * g
        top = d[g]
        t = {}
        for j in range(8):
            cj = jnp.broadcast_to(top[:, c0 + j : c0 + j + 1], (8, 128))
            for i in range(j, 8):
                t[i, j] = jnp.take_along_axis(cj, jnp.full((8, 128), i, jnp.int32), axis=0)
        for p in range(0, 8, 2):
            q = p + 1
            e = 1.0 / (t[p, p] * t[q, q] - t[q, p] * t[q, p])
            epp, eqq, eqp = t[q, q] * e, t[p, p] * e, t[q, p] * e
            rest = [i for i in range(8) if i not in (p, q)]
            cp = {i: t[max(i, p), min(i, p)] for i in rest}
            cq = {i: t[max(i, q), min(i, q)] for i in rest}
            lp = {i: (cp[i] * t[q, q] - cq[i] * t[q, p]) * e for i in rest}
            lq = {i: (cq[i] * t[p, p] - cp[i] * t[q, p]) * e for i in rest}
            for i in rest:
                for k in rest:
                    if k <= i:
                        t[i, k] = t[i, k] - (lp[i] * cp[k] + lq[i] * cq[k])
            for i in rest:
                t[max(i, p), min(i, p)] = lp[i]
                t[max(i, q), min(i, q)] = lq[i]
            t[p, p], t[q, q], t[q, p] = -epp, -eqq, eqp

        def column(j):
            e = [t[max(i, j), min(i, j)] for i in range(8)]
            even = (sub & 1) == 0
            e = [jnp.where(even, e[2 * i], e[2 * i + 1]) for i in range(4)]
            low = (sub & 2) == 0
            e = [jnp.where(low, e[0], e[1]), jnp.where(low, e[2], e[3])]
            return jnp.where(sub < 4, e[0], e[1])

        inside = (lane >= c0) & (lane < c0 + 8)
        unit = [
            jnp.where(
                inside,
                jnp.where(lane == c0 + j, 1.0, 0.0),
                jnp.broadcast_to(top[j : j + 1, :], (8, 128)),
            )
            for j in range(8)
        ]
        new = tree([column(j) * unit[j] for j in range(8)])
        spread = [jnp.broadcast_to(new[j : j + 1, :], (8, 128)) for j in range(8)]
        for i in list(range(g + 1, n)) + list(range(g)):
            old = d[i]
            d[i] = jnp.where(inside, 0.0, old) + tree(
                [jnp.broadcast_to(old[:, c0 + j : c0 + j + 1], (8, 128)) * spread[j] for j in range(8)]
            )
        d[g] = -new
    return d


def invert_block(d, lane, sub):
    wide = lax.broadcasted_iota(jnp.int32, (64, 128), 1)

    def body(s, carry):
        slab = sweep_slab([d[8 * i : 8 * i + 8, :] for i in range(8)], lane, sub)
        slab = jnp.concatenate(slab, axis=0)
        a, b, c = split3(jnp.concatenate([slab, jnp.zeros((64, 128), f32)], axis=0))
        rest = d[64:, :]
        rest = jnp.where(wide < 64, 0.0, rest) - dot(
            stack_left(rest), jnp.concatenate([a, b, a, c, a, b], axis=0), NN
        )
        d[:64, :] = pltpu.roll(rest, 64, 1)
        d[64:, :] = pltpu.roll(slab, 64, 1)
        return carry

    lax.fori_loop(0, 2, body, 0)


def stack_left(x):
    a, b, c = split3(x)
    return jnp.concatenate([a, a, b, a, c, b], axis=1)


def stack_right(x):
    a, b, c = split3(x)
    return jnp.concatenate([a, b, a, c, a, b], axis=1)


def solve_kernel(meta, own, other, fh_in, fl_in, residual, weights, new_weights, new_residual, p, dinv, us, fh, fl, sem, fsem):
    core = meta[1]
    pieces = []
    for side, src in enumerate((own, other)):
        half = core if side == 0 else 1 - core
        for s in range(4):
            row = half * HALF + ((meta[2 + side] + 4 - s) % 4) * QUART
            row = pl.multiple_of(row, 8)
            pieces.append(pltpu.make_async_copy(src.at[s], p.at[pl.ds(row, QUART)], sem))
    later = [pltpu.make_async_copy(fh_in, fh, fsem), pltpu.make_async_copy(fl_in, fl, fsem)]
    for c in pieces + later:
        c.start()
    for c in pieces:
        c.wait()
    lane = lax.broadcasted_iota(jnp.int32, (8, 128), 1)
    sub = lax.broadcasted_iota(jnp.int32, (8, 128), 0)
    eye = jnp.where(
        lax.broadcasted_iota(jnp.int32, (128, 128), 0) == lax.broadcasted_iota(jnp.int32, (128, 128), 1),
        ridge_weight,
        0.0,
    )
    def panel(k, carry):
        o = pl.multiple_of(k * (FB + PAD) - 64 * k * (k - 1), 8)
        dinv[...] = p[pl.ds(o, 128), :] + eye
        invert_block(dinv, lane, sub)
        for which in range(NB):
            pl.when(k == which)(lambda which=which: trailing(which))
        return carry

    def trailing(k):
        o = OFF[k]
        m = (NB - 1 - k) * 128 + PAD
        below = p[o + 128 : o + 128 + m, :]
        gain = dot(stack_left(below), stack_right(dinv[...]), NT)
        if k < NB - 1:
            left = stack_left(gain)
            right = stack_right(below[: m - PAD])
            j = k + 1
            if (NB - j) % 2:
                p[OFF[j] : OFF[j] + m, :] = p[OFF[j] : OFF[j] + m, :] - dot(left, right[:128], NT)
                j += 1
            while j < NB:
                b = (j - k - 1) * 128
                n = m - b
                both = dot(left[b:], right[b : b + 256], NT)
                p[OFF[j] : OFF[j] + n, :] = p[OFF[j] : OFF[j] + n, :] - both[:, :128]
                n -= 128
                p[OFF[j + 1] : OFF[j + 1] + n, :] = p[OFF[j + 1] : OFF[j + 1] + n, :] - both[128:, 128:]
                j += 2
        p[o + 128 : o + 128 + m, :] = gain

    lax.fori_loop(0, NB, panel, 0)
    u = [None] * NB
    for k in reversed(range(NB)):
        o = OFF[k]
        m = (NB - 1 - k) * 128
        acc = p[o + 128 + m : o + 128 + m + PAD, :]
        if k < NB - 1:
            done = jnp.concatenate(u[k + 1 :], axis=1)
            acc = acc - lax.dot_general(
                done,
                p[o + 128 : o + 128 + m, :],
                NN,
                precision=lax.Precision.HIGHEST,
                preferred_element_type=f32,
            )
        u[k] = acc
        us[k] = acc
    full = jnp.concatenate(u, axis=1)
    uh, ul = split2(full)
    new_weights[...] = weights[...] + us[meta[0]][:C]
    for c in later:
        c.wait()
    fit = dot(uh, fh[...], NN) + dot(uh, fl[...], NN) + dot(ul, fh[...], NN)
    new_residual[...] = residual[...] - fit[:C]


def x_perm(s):
    return [(f, ((f // 2 + s) % 4) * 2 + f % 2) for f in range(8)]


BOTH = ("feat", "rows")


def device_of(x, y, z, c):
    return (2 * x + c) * 32 + 8 * y + z


def ring_perm(s):
    pairs = []
    for x in range(4):
        for y in range(4):
            for z in range(8):
                pairs.append((device_of(x, y, z, 0), device_of((x + s) % 4, y, z, 0)))
                pairs.append((device_of(x, y, z, 1), device_of(x, (y + s) % 4, z, 1)))
    return pairs


GROUPS = [[device_of(x, y, z, 0) for y in range(4) for z in range(8)] for x in range(4)] + [
    [device_of(x, y, z, 1) for x in range(4) for z in range(8)] for y in range(4)
]

core_swap = [(f, f ^ 1) for f in range(8)]


def per_device(samples, residual, bank, bank_phase, bank_weights, block_index):
    chosen = block_index[0]
    feat = lax.axis_index("feat")
    rows = lax.axis_index("rows")
    x, core = feat // 2, feat % 2
    y = rows // 8
    block = jnp.concatenate(
        [
            lax.dynamic_index_in_dim(bank, chosen, 0, keepdims=False),
            lax.dynamic_index_in_dim(bank_phase, chosen, 0, keepdims=True),
            jnp.zeros((7, 128), f32),
        ],
        axis=0,
    )
    local_weights = lax.dynamic_index_in_dim(bank_weights, chosen, 0, keepdims=False)
    mine = jnp.stack([block] + [lax.ppermute(block, "feat", x_perm(s)) for s in (1, 2, 3)])
    theirs = lax.ppermute(mine, "feat", core_swap)
    proj = jnp.concatenate([mine, theirs], axis=0)
    order = [
        (x + 4 - f // 2) % 4 + jnp.where(core == f % 2, 0, 4) for f in range(8)
    ]
    meta = jnp.stack(order + [jnp.where(rows == 0, feat, -1), core]).astype(jnp.int32)
    smem = pl.BlockSpec(memory_space=pltpu.SMEM)
    vmem = pl.BlockSpec(memory_space=pltpu.VMEM)
    hbm = pl.BlockSpec(memory_space=pl.ANY)
    packed, fh, fl = pl.pallas_call(
        gram_kernel,
        out_shape=(
            jax.ShapeDtypeStruct((2, HALF, 128), f32),
            jax.ShapeDtypeStruct((FB, COLS), bf16),
            jax.ShapeDtypeStruct((FB, COLS), bf16),
        ),
        in_specs=[smem, vmem, vmem, vmem, vmem],
        out_specs=(vmem, vmem, vmem),
        compiler_params=pltpu.CompilerParams(vmem_limit_bytes=56 << 20),
        name="features_gram",
    )(meta, proj, samples, residual, local_weights)

    spot = jnp.where(core == 0, x, y)
    half = packed[0] + lax.ppermute(packed[1], "feat", core_swap)
    quarters = half.reshape(4, QUART, 128)
    got = [
        lax.ppermute(
            lax.dynamic_index_in_dim(quarters, (spot + s) % 4, 0, keepdims=False), BOTH, ring_perm(s)
        )
        for s in (1, 2, 3)
    ]
    quarter = lax.dynamic_index_in_dim(quarters, spot, 0, keepdims=False) + got[0] + got[1] + got[2]
    spread = jnp.pad(quarter, ((0, 32 * CHUNK - QUART), (0, 0))).reshape(32, CHUNK, 128)
    chunk = jnp.sum(lax.all_to_all(spread, BOTH, 0, 0, axis_index_groups=GROUPS), axis=0)
    full = lax.all_to_all(
        jnp.broadcast_to(chunk[None], (32, CHUNK, 128)), BOTH, 0, 0, axis_index_groups=GROUPS
    )
    quarter = full.reshape(32 * CHUNK, 128)[:QUART]
    own = jnp.stack([quarter] + [lax.ppermute(quarter, BOTH, ring_perm(s)) for s in (1, 2, 3)])
    other = lax.ppermute(own, "feat", core_swap)

    where = jnp.stack([feat, core, spot, jnp.where(core == 0, y, x)]).astype(jnp.int32)
    new_weights, new_residual = pl.pallas_call(
        solve_kernel,
        out_shape=(
            jax.ShapeDtypeStruct((C, 128), f32),
            jax.ShapeDtypeStruct((C, COLS), f32),
        ),
        in_specs=[smem, hbm, hbm, hbm, hbm, vmem, vmem],
        out_specs=(vmem, vmem),
        scratch_shapes=[
            pltpu.VMEM((T, 128), f32),
            pltpu.VMEM((128, 128), f32),
            pltpu.VMEM((NB, PAD, 128), f32),
            pltpu.VMEM((FB, COLS), bf16),
            pltpu.VMEM((FB, COLS), bf16),
            pltpu.SemaphoreType.DMA,
            pltpu.SemaphoreType.DMA,
        ],
        compiler_params=pltpu.CompilerParams(vmem_limit_bytes=56 << 20),
        name="block_solve",
    )(where, own, other, fh, fl, residual, local_weights)
    return (new_weights, new_residual)


def solution(mesh):
    in_specs = (
        P(None, ("feat", "rows")),
        P(None, ("feat", "rows")),
        P(None, None, "feat"),
        P(None, "feat"),
        P(None, None, "feat"),
        P(),
    )
    out_specs = (P(None, "feat"), P(None, ("feat", "rows")))
    return jax.shard_map(
        per_device, mesh=mesh, in_specs=in_specs, out_specs=out_specs, check_vma=False
    )
```

profile of v0, /device:TPU:1, one launch (start us, length us, event | category | flops | bytes accessed | tf_op | source)
XLA Modules:
  0.0 172.0 jit_solution(2753820381568316107)
XLA Ops:
  1.4 0.7 constant_dynamic-slice_fusion.1
  2.4 2.1 %collective-permute-start = (f32[448,128]{1,0:T(8,128)S(1)}, f32[448,128]{1,0:T(8,128)S(1)}, u32[]{:S(2)}, u32[]{:S(2)}) collective-permute-start(f32[448,128]{1,0:T(8,128)S(1)} %get-tuple-element.14), channel_id=1, source_target_pairs={{0,64},{32,96},{64,128},{96,160},{128,192},{160,224},{192,0},{224,... | collective-permute-start | bytes 688136 | tf_op jit(solution)/shard_map/ppermute | solution.py:299
  4.5 2.5 %collective-permute-start.1 = (f32[448,128]{1,0:T(8,128)S(1)}, f32[448,128]{1,0:T(8,128)S(1)}, u32[]{:S(2)}, u32[]{:S(2)}) collective-permute-start(f32[448,128]{1,0:T(8,128)S(1)} %get-tuple-element.14), channel_id=1, source_target_pairs={{0,128},{32,160},{64,192},{96,224},{128,0},{160,32},{192,64},{224,... | collective-permute-start | bytes 688136 | tf_op jit(solution)/shard_map/ppermute | solution.py:299
  6.9 1.2 collective-permute-start.2
  8.1 1.1 constant_dynamic-slice_fusion
  9.2 0.6 copy.11
  9.9 0.7 stack.90.meta
  10.5 6.3 %collective-permute-done.1 = f32[448,128]{1,0:T(8,128)S(1)} collective-permute-done((f32[448,128]{1,0:T(8,128)S(1)}, f32[448,128]{1,0:T(8,128)S(1)}, u32[]{:S(2)}, u32[]{:S(2)}) %collective-permute-start.1) | collective-permute-done | bytes 229408 | tf_op jit(solution)/shard_map/ppermute | solution.py:299
  16.9 1.8 %collective-permute-start.3 = (f32[4,448,128]{2,1,0:T(8,128)S(1)}, f32[4,448,128]{2,1,0:T(8,128)S(1)}, u32[]{:S(2)}, u32[]{:S(2)}) collective-permute-start(f32[4,448,128]{2,1,0:T(8,128)S(1)} %pad_maximum_fusion.1), channel_id=1, source_target_pairs={{0,32},{32,0},{64,96},{96,64},{128,160},{160,128},{192,224},{224,1... | collective-permute-start | bytes 2752520 | tf_op jit(solution)/shard_map/ppermute | solution.py:300
  18.9 1.9 %collective-permute-done.3 = f32[4,448,128]{2,1,0:T(8,128)S(1)} collective-permute-done((f32[4,448,128]{2,1,0:T(8,128)S(1)}, f32[4,448,128]{2,1,0:T(8,128)S(1)}, u32[]{:S(2)}, u32[]{:S(2)}) %collective-permute-start.3) | collective-permute-done | bytes 917536 | tf_op jit(solution)/shard_map/ppermute | solution.py:300
  20.9 1.3 copy-done.2
  22.2 13.7 %features_gram.1 = (f32[2,2912,128]{2,1,0:T(8,128)}, bf16[1024,1024]{1,0:T(8,128)(2,1)}, bf16[1024,1024]{1,0:T(8,128)(2,1)}) custom-call(s32[10]{0:T(128)} %stack.90.meta, f32[8,448,128]{2,1,0:T(8,128)} %copy-done.2, f32[440,1024]{1,0:T(8,128)} %samples.1, f32[147,1024]{1,0:T(8,128)} %residual.3, f32[147,128]{1,0:T(8,128)} %bitcast.62), custom_call_target="tpu_custom_call" | custom-call | tf_op jit(solution)/shard_map/features_gram/pallas_call | solution.py:309
  35.9 1.5 slice_bitcast_fusion
  37.4 0.5 collective-permute-start.4
  37.8 3.1 %collective-permute-done.4 = f32[2912,128]{1,0:T(8,128)} collective-permute-done((f32[2912,128]{1,0:T(8,128)S(1)}, f32[2912,128]{1,0:T(8,128)}, u32[]{:S(2)}, u32[]{:S(2)}) %collective-permute-start.4) | collective-permute-done | bytes 1490976 | tf_op jit(solution)/shard_map/ppermute | solution.py:323
  40.9 2.0 %bitcast_add_fusion = f32[2912,128]{1,0:T(8,128)S(1)} fusion(f32[2912,128]{1,0:T(8,128)} %collective-permute-done.4, f32[2,2912,128]{2,1,0:T(8,128)} %get-tuple-element.5), kind=kLoop, calls=%fused_computation.1 | loop fusion | flops 372736 | bytes 4472832 | tf_op jit(solution)/shard_map/add | solution.py:323
  42.9 1.0 dynamic-slice_bitcast_fusion.2
  43.9 2.7 %collective-permute-start.7 = (f32[728,128]{1,0:T(8,128)}, f32[728,128]{1,0:T(8,128)}, u32[]{:S(2)}, u32[]{:S(2)}) collective-permute-start(f32[728,128]{1,0:T(8,128)} %get-tuple-element.9), channel_id=1, source_target_pairs={{0,192},{32,56},{1,193},{33,57},{2,194},{34,58},{3,195},{35,59},{4... | collective-permute-start | bytes 1118216 | tf_op jit(solution)/shard_map/ppermute | solution.py:326
  47.0 0.7 collective-permute-start.5
  47.7 7.8 %collective-permute-done.7 = f32[728,128]{1,0:T(8,128)} collective-permute-done((f32[728,128]{1,0:T(8,128)}, f32[728,128]{1,0:T(8,128)}, u32[]{:S(2)}, u32[]{:S(2)}) %collective-permute-start.7) | collective-permute-done | bytes 372768 | tf_op jit(solution)/shard_map/ppermute | solution.py:326
  55.5 3.7 %collective-permute-done.5 = f32[728,128]{1,0:T(8,128)} collective-permute-done((f32[728,128]{1,0:T(8,128)}, f32[728,128]{1,0:T(8,128)}, u32[]{:S(2)}, u32[]{:S(2)}) %collective-permute-start.5) | collective-permute-done | bytes 372768 | tf_op jit(solution)/shard_map/ppermute | solution.py:326
  59.2 1.3 fusion.1
  60.5 24.9 %all_to_all.10 = f32[32,24,128]{2,1,0:T(8,128)S(1)} all-to-all(f32[32,24,128]{2,1,0:T(8,128)S(1)} %bitcast.57), channel_id=1, replica_groups={{0,1,2,3,4,5,6,7,8,9,10,11,12,13,14,15,16,17,18,19,20,21,22,23,24,25,26..., dimensions={0} | all-to-all | bytes 786432 | tf_op jit(solution)/shard_map/all_to_all | solution.py:333
  85.5 17.1 %all_to_all.11 = f32[32,24,128]{2,1,0:T(8,128)S(1)} all-to-all(f32[32,24,128]{2,1,0:T(8,128)S(1)} %broadcast_in_dim.10), channel_id=1, replica_groups={{0,1,2,3,4,5,6,7,8,9,10,11,12,13,14,15,16,17,18,19,20,21,22,23,24,25,26..., dimensions={0} | all-to-all | bytes 786432 | tf_op jit(solution)/shard_map/all_to_all | solution.py:334
  102.8 1.4 collective-permute-start.8
  104.2 5.2 %collective-permute-done.10 = f32[728,128]{1,0:T(8,128)S(1)} collective-permute-done((f32[728,128]{1,0:T(8,128)S(1)}, f32[728,128]{1,0:T(8,128)S(1)}, u32[]{:S(2)}, u32[]{:S(2)}) %collective-permute-start.10) | collective-permute-done | bytes 372768 | tf_op jit(solution)/shard_map/ppermute | solution.py:338
  109.4 1.4 collective-permute-done.9
  110.8 4.2 %collective-permute-done.8 = f32[728,128]{1,0:T(8,128)S(1)} collective-permute-done((f32[728,128]{1,0:T(8,128)S(1)}, f32[728,128]{1,0:T(8,128)S(1)}, u32[]{:S(2)}, u32[]{:S(2)}) %collective-permute-start.8) | collective-permute-done | bytes 372768 | tf_op jit(solution)/shard_map/ppermute | solution.py:338
  115.2 5.0 %collective-permute-start.11 = (f32[4,728,128]{2,1,0:T(8,128)S(1)}, f32[4,728,128]{2,1,0:T(8,128)}, u32[]{:S(2)}, u32[]{:S(2)}) collective-permute-start(f32[4,728,128]{2,1,0:T(8,128)S(1)} %pad_maximum_fusion.own), channel_id=1, source_target_pairs={{0,32},{32,0},{64,96},{96,64},{128,160},{160,128},{192,224},{224,1... | collective-permute-start | bytes 4472840 | tf_op jit(solution)/shard_map/ppermute | solution.py:339
  120.2 0.6 pad_add_fusion.meta
  120.8 2.4 %collective-permute-done.11.other = f32[4,728,128]{2,1,0:T(8,128)} collective-permute-done((f32[4,728,128]{2,1,0:T(8,128)S(1)}, f32[4,728,128]{2,1,0:T(8,128)}, u32[]{:S(2)}, u32[]{:S(2)}) %collective-permute-start.11) | collective-permute-done | bytes 1490976 | tf_op jit(solution)/shard_map/ppermute | solution.py:339
  123.2 48.5 %block_solve.1 = (f32[147,128]{1,0:T(8,128)}, f32[147,1024]{1,0:T(8,128)}) custom-call(s32[4]{0:T(128)} %pad_add_fusion.meta, f32[4,728,128]{2,1,0:T(8,128)} %copy-done.1, f32[4,728,128]{2,1,0:T(8,128)} %collective-permute-done.11.other, bf16[1024,1024]{1,0:T(8,128)(2,1)} %get-tuple-element.6.fh_in, bf16[1024,1024]{1,0:T(8,128)(2,1)} %get-tuple-element.7.fl_in, ...), custom_call_target="tpu_custom_call" | custom-call | tf_op jit(solution)/shard_map/block_solve/pallas_call | solution.py:342
  (26 shorter events, 1.4 us)
Async XLA Ops:
  0.6 1.5 copy-start
  2.4 8.1 %collective-permute-start = (f32[448,128]{1,0:T(8,128)S(1)}, f32[448,128]{1,0:T(8,128)S(1)}, u32[]{:S(2)}, u32[]{:S(2)}) collective-permute-start(f32[448,128]{1,0:T(8,128)S(1)} %get-tuple-element.14), channel_id=1, source_target_pairs={{0,64},{32,96},{64,128},{96,160},{128,192},{160,224},{192,0},{224,... | collective-permute-start | bytes 688136 | tf_op jit(solution)/shard_map/ppermute | solution.py:299
  4.5 12.4 %collective-permute-start.1 = (f32[448,128]{1,0:T(8,128)S(1)}, f32[448,128]{1,0:T(8,128)S(1)}, u32[]{:S(2)}, u32[]{:S(2)}) collective-permute-start(f32[448,128]{1,0:T(8,128)S(1)} %get-tuple-element.14), channel_id=1, source_target_pairs={{0,128},{32,160},{64,192},{96,224},{128,0},{160,32},{192,64},{224,... | collective-permute-start | bytes 688136 | tf_op jit(solution)/shard_map/ppermute | solution.py:299
  6.9 9.9 %collective-permute-start.2 = (f32[448,128]{1,0:T(8,128)S(1)}, f32[448,128]{1,0:T(8,128)S(1)}, u32[]{:S(2)}, u32[]{:S(2)}) collective-permute-start(f32[448,128]{1,0:T(8,128)S(1)} %get-tuple-element.14), channel_id=1, source_target_pairs={{0,192},{32,224},{64,0},{96,32},{128,64},{160,96},{192,128},{224,1... | collective-permute-start | bytes 688136 | tf_op jit(solution)/shard_map/ppermute | solution.py:299
  16.9 3.9 %collective-permute-start.3 = (f32[4,448,128]{2,1,0:T(8,128)S(1)}, f32[4,448,128]{2,1,0:T(8,128)S(1)}, u32[]{:S(2)}, u32[]{:S(2)}) collective-permute-start(f32[4,448,128]{2,1,0:T(8,128)S(1)} %pad_maximum_fusion.1), channel_id=1, source_target_pairs={{0,32},{32,0},{64,96},{96,64},{128,160},{160,128},{192,224},{224,1... | collective-permute-start | bytes 2752520 | tf_op jit(solution)/shard_map/ppermute | solution.py:300
  20.9 1.3 copy-start.2
  37.4 3.5 %collective-permute-start.4 = (f32[2912,128]{1,0:T(8,128)S(1)}, f32[2912,128]{1,0:T(8,128)}, u32[]{:S(2)}, u32[]{:S(2)}) collective-permute-start(f32[2912,128]{1,0:T(8,128)S(1)} %slice_bitcast_fusion), channel_id=1, source_target_pairs={{0,32},{32,0},{64,96},{96,64},{128,160},{160,128},{192,224},{224,1... | collective-permute-start | bytes 4472840 | tf_op jit(solution)/shard_map/ppermute | solution.py:323
  43.9 11.5 %collective-permute-start.7 = (f32[728,128]{1,0:T(8,128)}, f32[728,128]{1,0:T(8,128)}, u32[]{:S(2)}, u32[]{:S(2)}) collective-permute-start(f32[728,128]{1,0:T(8,128)} %get-tuple-element.9), channel_id=1, source_target_pairs={{0,192},{32,56},{1,193},{33,57},{2,194},{34,58},{3,195},{35,59},{4... | collective-permute-start | bytes 1118216 | tf_op jit(solution)/shard_map/ppermute | solution.py:326
  46.6 8.8 %collective-permute-start.6 = (f32[728,128]{1,0:T(8,128)}, f32[728,128]{1,0:T(8,128)}, u32[]{:S(2)}, u32[]{:S(2)}) collective-permute-start(f32[728,128]{1,0:T(8,128)} %get-tuple-element.10), channel_id=1, source_target_pairs={{0,128},{32,48},{1,129},{33,49},{2,130},{34,50},{3,131},{35,51},{4... | collective-permute-start | bytes 1118216 | tf_op jit(solution)/shard_map/ppermute | solution.py:326
  47.0 12.2 %collective-permute-start.5 = (f32[728,128]{1,0:T(8,128)}, f32[728,128]{1,0:T(8,128)}, u32[]{:S(2)}, u32[]{:S(2)}) collective-permute-start(f32[728,128]{1,0:T(8,128)} %get-tuple-element.8), channel_id=1, source_target_pairs={{0,64},{32,40},{1,65},{33,41},{2,66},{34,42},{3,67},{35,43},{4,68}... | collective-permute-start | bytes 1118216 | tf_op jit(solution)/shard_map/ppermute | solution.py:326
  102.7 6.8 %collective-permute-start.10 = (f32[728,128]{1,0:T(8,128)S(1)}, f32[728,128]{1,0:T(8,128)S(1)}, u32[]{:S(2)}, u32[]{:S(2)}) collective-permute-start(f32[728,128]{1,0:T(8,128)S(1)} %get-tuple-element.12), channel_id=1, source_target_pairs={{0,192},{32,56},{1,193},{33,57},{2,194},{34,58},{3,195},{35,59},{4... | collective-permute-start | bytes 1118216 | tf_op jit(solution)/shard_map/ppermute | solution.py:338
  102.7 8.1 %collective-permute-start.9 = (f32[728,128]{1,0:T(8,128)S(1)}, f32[728,128]{1,0:T(8,128)S(1)}, u32[]{:S(2)}, u32[]{:S(2)}) collective-permute-start(f32[728,128]{1,0:T(8,128)S(1)} %get-tuple-element.12), channel_id=1, source_target_pairs={{0,128},{32,48},{1,129},{33,49},{2,130},{34,50},{3,131},{35,51},{4... | collective-permute-start | bytes 1118216 | tf_op jit(solution)/shard_map/ppermute | solution.py:338
  102.8 12.2 %collective-permute-start.8 = (f32[728,128]{1,0:T(8,128)S(1)}, f32[728,128]{1,0:T(8,128)S(1)}, u32[]{:S(2)}, u32[]{:S(2)}) collective-permute-start(f32[728,128]{1,0:T(8,128)S(1)} %get-tuple-element.12), channel_id=1, source_target_pairs={{0,64},{32,40},{1,65},{33,41},{2,66},{34,42},{3,67},{35,43},{4,68}... | collective-permute-start | bytes 1118216 | tf_op jit(solution)/shard_map/ppermute | solution.py:338
  115.2 8.0 %copy-start.1 = (f32[4,728,128]{2,1,0:T(8,128)}, f32[4,728,128]{2,1,0:T(8,128)S(1)}, u32[]{:S(2)}) copy-start(f32[4,728,128]{2,1,0:T(8,128)S(1)} %pad_maximum_fusion.own) | copy-start | bytes 4472836
  115.2 8.0 %collective-permute-start.11 = (f32[4,728,128]{2,1,0:T(8,128)S(1)}, f32[4,728,128]{2,1,0:T(8,128)}, u32[]{:S(2)}, u32[]{:S(2)}) collective-permute-start(f32[4,728,128]{2,1,0:T(8,128)S(1)} %pad_maximum_fusion.own), channel_id=1, source_target_pairs={{0,32},{32,0},{64,96},{96,64},{128,160},{160,128},{192,224},{224,1... | collective-permute-start | bytes 4472840 | tf_op jit(solution)/shard_map/ppermute | solution.py:339
where the time goes:
time: 172 us
  Pallas kernels  62.2 us (36%)
  blocking collectives  42 us (24%)
  waiting for transfers between devices  36.1 us (21%)
  starting transfers between devices  18.2 us (11%)
  local copies, waits for them, and re-layouts  7.26 us (4%)
  other arithmetic  4.38 us (3%)
  between operations  1.76 us (1%)
    pallas_call x1, Pallas kernels, per_device(): pl.pallas_call(solve_kernel, out_shape=(jax.ShapeDtypeStruct((C, 128), f3...  48.5 us
    all_to_all x1, blocking collectives, per_device(): lax.all_to_all(spread, BOTH, 0, 0, axis_index_groups=GROUPS)  24.9 us
    all_to_all x1, blocking collectives, per_device(): lax.all_to_all(jnp.broadcast_to(chunk[None], (32, CHUNK, 128)), BOTH, 0,...  17.1 us
    pallas_call x1, Pallas kernels, per_device(): pl.pallas_call(gram_kernel, out_shape=(jax.ShapeDtypeStruct((2, HALF, 128...  13.7 us
    ppermute x3, waiting for transfers between devices, per_device(): lax.ppermute(lax.dynamic_index_in_dim(quarters, (spot + s) % 4, 0, keepdi...  11.5 us
    ppermute x3, waiting for transfers between devices, per_device(): lax.ppermute(quarter, BOTH, ring_perm(s))  10.8 us
    ppermute x3, waiting for transfers between devices, per_device(): lax.ppermute(block, 'feat', x_perm(s))  6.36 us
    ppermute x3, starting transfers between devices, per_device(): lax.ppermute(block, 'feat', x_perm(s))  5.71 us
  transfers between devices with their start and end apart: 12, of which 9 were waited for; matrix products, arithmetic and copies ran while one was open for 2% of the time, Pallas kernels for 0%

commit v1 on v0

--- a/solution.py
+++ b/solution.py
@@ -43,9 +43,26 @@
     return a, b, (r - b.astype(f32)).astype(bf16)
 
 
-def gram_kernel(meta, proj, samples, residual, weights, packed, fh, fl):
+def gram_kernel(
+    meta, mine, theirs, samples_in, residual_in, weights_in, keep, give, fh_out, fl_out,
+    proj, samples, residual, weights, packed, fh, fl, sem,
+):
+    first = pltpu.make_async_copy(samples_in, samples, sem.at[0])
+    blocks = [
+        pltpu.make_async_copy(mine, proj.at[0:4], sem.at[1]),
+        pltpu.make_async_copy(theirs, proj.at[4:8], sem.at[2]),
+    ]
+    rest = [
+        pltpu.make_async_copy(residual_in, residual, sem.at[3]),
+        pltpu.make_async_copy(weights_in, weights, sem.at[4]),
+    ]
+    for c in [first] + blocks + rest:
+        c.start()
+    first.wait()
     s = jnp.concatenate([samples[...], jnp.zeros((8, COLS), f32)], axis=0)
     sh, sl = split2(s)
+    for c in blocks:
+        c.wait()
     for f in range(8):
         turned = (proj[meta[f]] * TURN).T
         h, l = split2(turned)
@@ -58,6 +75,14 @@
         ch, cl = split2(c)
         fh[128 * f : 128 * f + 128, :] = ch
         fl[128 * f : 128 * f + 128, :] = cl
+    out = [
+        pltpu.make_async_copy(fh, fh_out, sem.at[0]),
+        pltpu.make_async_copy(fl, fl_out, sem.at[1]),
+    ]
+    for c in out:
+        c.start()
+    for c in rest:
+        c.wait()
     rh, rl = split2(jnp.concatenate([residual[...], jnp.zeros((PAD - C, COLS), f32)], axis=0))
     inv = 1.0 / (COLS * 256)
 
@@ -81,6 +106,14 @@
             put(OFF[k], g[128 * j :, 128 * j : 128 * j + 128])
             own = jnp.where(meta[8] == k, 1.0, 0.0)
             put(OFF[k] + m, r[:, 128 * j : 128 * j + 128] + ridge * own)
+    out = out + [
+        pltpu.make_async_copy(packed.at[1], give, sem.at[2]),
+        pltpu.make_async_copy(packed.at[0], keep, sem.at[3]),
+    ]
+    for c in out[2:]:
+        c.start()
+    for c in out:
+        c.wait()
 
 
 def tree(xs):
@@ -209,7 +242,18 @@
         o = OFF[k]
         m = (NB - 1 - k) * 128 + PAD
         below = p[o + 128 : o + 128 + m, :]
-        gain = dot(stack_left(below), stack_right(dinv[...]), NT)
+        a, b, c = split3(below)
+        da, db, dc = split3(dinv[...])
+        zero = jnp.zeros((128, 128), bf16)
+        wide = jnp.concatenate(
+            [
+                jnp.concatenate([da, da, da, zero], axis=1),
+                jnp.concatenate([db, db, zero, dc], axis=1),
+            ],
+            axis=0,
+        )
+        gain = dot(jnp.concatenate([a, b, c, a], axis=1), wide, NT)
+        gain = gain[:, :128] + gain[:, 128:]
         if k < NB - 1:
             left = stack_left(gain)
             right = stack_right(below[: m - PAD])
@@ -297,30 +341,41 @@
     )
     local_weights = lax.dynamic_index_in_dim(bank_weights, chosen, 0, keepdims=False)
     mine = jnp.stack([block] + [lax.ppermute(block, "feat", x_perm(s)) for s in (1, 2, 3)])
-    theirs = lax.ppermute(mine, "feat", core_swap)
-    proj = jnp.concatenate([mine, theirs], axis=0)
     order = [
         (x + 4 - f // 2) % 4 + jnp.where(core == f % 2, 0, 4) for f in range(8)
     ]
     meta = jnp.stack(order + [jnp.where(rows == 0, feat, -1), core]).astype(jnp.int32)
+    mine, meta, local_weights = lax.optimization_barrier((mine, meta, local_weights))
+    theirs = lax.ppermute(mine, "feat", core_swap)
     smem = pl.BlockSpec(memory_space=pltpu.SMEM)
     vmem = pl.BlockSpec(memory_space=pltpu.VMEM)
     hbm = pl.BlockSpec(memory_space=pl.ANY)
-    packed, fh, fl = pl.pallas_call(
+    keep, give, fh, fl = pl.pallas_call(
         gram_kernel,
         out_shape=(
-            jax.ShapeDtypeStruct((2, HALF, 128), f32),
+            jax.ShapeDtypeStruct((HALF, 128), f32),
+            jax.ShapeDtypeStruct((HALF, 128), f32),
             jax.ShapeDtypeStruct((FB, COLS), bf16),
             jax.ShapeDtypeStruct((FB, COLS), bf16),
         ),
-        in_specs=[smem, vmem, vmem, vmem, vmem],
-        out_specs=(vmem, vmem, vmem),
+        in_specs=[smem, hbm, hbm, hbm, hbm, hbm],
+        out_specs=(hbm, hbm, hbm, hbm),
+        scratch_shapes=[
+            pltpu.VMEM((8, 448, 128), f32),
+            pltpu.VMEM((D, COLS), f32),
+            pltpu.VMEM((C, COLS), f32),
+            pltpu.VMEM((C, 128), f32),
+            pltpu.VMEM((2, HALF, 128), f32),
+            pltpu.VMEM((FB, COLS), bf16),
+            pltpu.VMEM((FB, COLS), bf16),
+            pltpu.SemaphoreType.DMA((5,)),
+        ],
         compiler_params=pltpu.CompilerParams(vmem_limit_bytes=56 << 20),
         name="features_gram",
-    )(meta, proj, samples, residual, local_weights)
+    )(meta, mine, theirs, samples, residual, local_weights)
 
     spot = jnp.where(core == 0, x, y)
-    half = packed[0] + lax.ppermute(packed[1], "feat", core_swap)
+    half = keep + lax.ppermute(give, "feat", core_swap)
     quarters = half.reshape(4, QUART, 128)
     got = [
         lax.ppermute(

time: 172 us -> 172 us (level)
  waiting for transfers between devices: 36.1 us -> 40 us
  starting transfers between devices: 18.2 us -> 16.3 us
    ppermute x3, waiting for transfers between devices: 6.36 us -> 10.4 us  [per_device(): lax.ppermute(block, 'feat', x_perm(s))]
    all_to_all x1, blocking collectives: 24.9 us -> 21.8 us  [per_device(): lax.all_to_all(spread, BOTH, 0, 0, axis_index_groups=GROUPS)]
  transfers between devices with their start and end apart: 12 -> 12, of which waited for: 9 -> 10; matrix products, arithmetic and copies ran while one was open for 2% -> 2% of each run, Pallas kernels for 0% -> 0%
where the time goes in v1:
time: 172 us
  Pallas kernels  62.1 us (36%)
  blocking collectives  40.6 us (24%)
  waiting for transfers between devices  40 us (23%)
  starting transfers between devices  16.3 us (9%)
  local copies, waits for them, and re-layouts  6.55 us (4%)
  other arithmetic  4.3 us (2%)
    pallas_call x1, Pallas kernels, per_device(): pl.pallas_call(solve_kernel, out_shape=(jax.ShapeDtypeStruct((C, 128), f3...  47.6 us
    all_to_all x1, blocking collectives, per_device(): lax.all_to_all(spread, BOTH, 0, 0, axis_index_groups=GROUPS)  21.8 us
    all_to_all x1, blocking collectives, per_device(): lax.all_to_all(jnp.broadcast_to(chunk[None], (32, CHUNK, 128)), BOTH, 0,...  18.8 us
    pallas_call x1, Pallas kernels, per_device(): pl.pallas_call(gram_kernel, out_shape=(jax.ShapeDtypeStruct((HALF, 128),...  14.5 us
    ppermute x3, waiting for transfers between devices, per_device(): lax.ppermute(lax.dynamic_index_in_dim(quarters, (spot + s) % 4, 0, keepdi...  11.2 us
    ppermute x3, waiting for transfers between devices, per_device(): lax.ppermute(quarter, BOTH, ring_perm(s))  10.8 us
    ppermute x3, waiting for transfers between devices, per_device(): lax.ppermute(block, 'feat', x_perm(s))  10.4 us
    ppermute x1, starting transfers between devices, per_device(): other = lax.ppermute(own, 'feat', core_swap)  5.28 us
  transfers between devices with their start and end apart: 12, of which 10 were waited for; matrix products, arithmetic and copies ran while one was open for 2% of the time, Pallas kernels for 0%

profile of v1, /device:TPU:1, one launch (start us, length us, event | category | flops | bytes accessed | tf_op | source)
XLA Modules:
  0.0 171.5 jit_solution(2526494939563928786)
XLA Ops:
  1.4 0.7 constant_dynamic-slice_fusion.1
  2.4 3.4 %collective-permute-start.2 = (f32[448,128]{1,0:T(8,128)S(1)}, f32[448,128]{1,0:T(8,128)S(1)}, u32[]{:S(2)}, u32[]{:S(2)}) collective-permute-start(f32[448,128]{1,0:T(8,128)S(1)} %get-tuple-element.22), channel_id=1, source_target_pairs={{0,192},{32,224},{64,0},{96,32},{128,64},{160,96},{192,128},{224,1... | collective-permute-start | bytes 688136 | tf_op jit(solution)/shard_map/ppermute | solution.py:343
  6.3 0.6 collective-permute-start
  6.9 1.1 constant_dynamic-slice_fusion
  8.0 0.6 copy.11
  8.6 0.7 stack.95.meta
  9.3 5.6 %collective-permute-done.2 = f32[448,128]{1,0:T(8,128)S(1)} collective-permute-done((f32[448,128]{1,0:T(8,128)S(1)}, f32[448,128]{1,0:T(8,128)S(1)}, u32[]{:S(2)}, u32[]{:S(2)}) %collective-permute-start.2) | collective-permute-done | bytes 229408 | tf_op jit(solution)/shard_map/ppermute | solution.py:343
  14.9 4.8 %collective-permute-done = f32[448,128]{1,0:T(8,128)S(1)} collective-permute-done((f32[448,128]{1,0:T(8,128)S(1)}, f32[448,128]{1,0:T(8,128)S(1)}, u32[]{:S(2)}, u32[]{:S(2)}) %collective-permute-start) | collective-permute-done | bytes 229408 | tf_op jit(solution)/shard_map/ppermute | solution.py:343
  19.8 0.6 collective-permute-start.3
  20.4 2.1 %collective-permute-done.3.theirs = f32[4,448,128]{2,1,0:T(8,128)S(1)} collective-permute-done((f32[4,448,128]{2,1,0:T(8,128)S(1)}, f32[4,448,128]{2,1,0:T(8,128)S(1)}, u32[]{:S(2)}, u32[]{:S(2)}) %collective-permute-start.3) | collective-permute-done | bytes 917536 | tf_op jit(solution)/shard_map/ppermute | solution.py:349
  22.5 1.0 copy-done.4
  23.5 14.5 %features_gram.1 = (f32[2912,128]{1,0:T(8,128)}, f32[2912,128]{1,0:T(8,128)}, bf16[1024,1024]{1,0:T(8,128)(2,1)}, bf16[1024,1024]{1,0:T(8,128)(2,1)}) custom-call(s32[10]{0:T(128)} %stack.95.meta, f32[4,448,128]{2,1,0:T(8,128)} %copy-done.2, f32[4,448,128]{2,1,0:T(8,128)} %copy-done.4, f32[440,1024]{1,0:T(8,128)} %samples_in.1, f32[147,1024]{1,0:T(8,128)} %residual.1, ...), custom_call_target="tpu_custom_call" | custom-call | tf_op jit(solution)/shard_map/features_gram/pallas_call | solution.py:353
  38.0 0.6 collective-permute-start.4
  38.6 3.1 %collective-permute-done.4 = f32[2912,128]{1,0:T(8,128)S(1)} collective-permute-done((f32[2912,128]{1,0:T(8,128)}, f32[2912,128]{1,0:T(8,128)S(1)}, u32[]{:S(2)}, u32[]{:S(2)}) %collective-permute-start.4) | collective-permute-done | bytes 1490976 | tf_op jit(solution)/shard_map/ppermute | solution.py:378
  41.7 1.2 copy-done.3
  42.9 2.0 %add.133 = f32[2912,128]{1,0:T(8,128)S(1)} add(f32[2912,128]{1,0:T(8,128)} %get-tuple-element.12, f32[2912,128]{1,0:T(8,128)} %copy-done.3) | non-fusion elementwise | flops 372736 | bytes 4472832 | tf_op jit(solution)/shard_map/add | solution.py:378
  44.9 1.0 dynamic-slice_bitcast_fusion.2
  45.9 2.7 %collective-permute-start.7 = (f32[728,128]{1,0:T(8,128)}, f32[728,128]{1,0:T(8,128)}, u32[]{:S(2)}, u32[]{:S(2)}) collective-permute-start(f32[728,128]{1,0:T(8,128)} %get-tuple-element.17), channel_id=1, source_target_pairs={{0,192},{32,56},{1,193},{33,57},{2,194},{34,58},{3,195},{35,59},{4... | collective-permute-start | bytes 1118216 | tf_op jit(solution)/shard_map/ppermute | solution.py:381
  49.0 0.7 collective-permute-start.5
  49.7 7.8 %collective-permute-done.7 = f32[728,128]{1,0:T(8,128)} collective-permute-done((f32[728,128]{1,0:T(8,128)}, f32[728,128]{1,0:T(8,128)}, u32[]{:S(2)}, u32[]{:S(2)}) %collective-permute-start.7) | collective-permute-done | bytes 372768 | tf_op jit(solution)/shard_map/ppermute | solution.py:381
  57.5 3.4 %collective-permute-done.5 = f32[728,128]{1,0:T(8,128)} collective-permute-done((f32[728,128]{1,0:T(8,128)}, f32[728,128]{1,0:T(8,128)}, u32[]{:S(2)}, u32[]{:S(2)}) %collective-permute-start.5) | collective-permute-done | bytes 372768 | tf_op jit(solution)/shard_map/ppermute | solution.py:381
  60.9 1.3 fusion.1
  62.2 21.8 %all_to_all.10 = f32[32,24,128]{2,1,0:T(8,128)S(1)} all-to-all(f32[32,24,128]{2,1,0:T(8,128)S(1)} %bitcast.49), channel_id=1, replica_groups={{0,1,2,3,4,5,6,7,8,9,10,11,12,13,14,15,16,17,18,19,20,21,22,23,24,25,26..., dimensions={0} | all-to-all | bytes 786432 | tf_op jit(solution)/shard_map/all_to_all | solution.py:388
  84.0 18.8 %all_to_all.11 = f32[32,24,128]{2,1,0:T(8,128)S(1)} all-to-all(f32[32,24,128]{2,1,0:T(8,128)S(1)} %broadcast_in_dim.10), channel_id=1, replica_groups={{0,1,2,3,4,5,6,7,8,9,10,11,12,13,14,15,16,17,18,19,20,21,22,23,24,25,26..., dimensions={0} | all-to-all | bytes 786432 | tf_op jit(solution)/shard_map/all_to_all | solution.py:389
  103.1 1.4 collective-permute-start.8
  104.4 5.2 %collective-permute-done.10 = f32[728,128]{1,0:T(8,128)S(1)} collective-permute-done((f32[728,128]{1,0:T(8,128)S(1)}, f32[728,128]{1,0:T(8,128)S(1)}, u32[]{:S(2)}, u32[]{:S(2)}) %collective-permute-start.10) | collective-permute-done | bytes 372768 | tf_op jit(solution)/shard_map/ppermute | solution.py:393
  109.7 1.4 collective-permute-done.9
  111.1 4.2 %collective-permute-done.8 = f32[728,128]{1,0:T(8,128)S(1)} collective-permute-done((f32[728,128]{1,0:T(8,128)S(1)}, f32[728,128]{1,0:T(8,128)S(1)}, u32[]{:S(2)}, u32[]{:S(2)}) %collective-permute-start.8) | collective-permute-done | bytes 372768 | tf_op jit(solution)/shard_map/ppermute | solution.py:393
  115.4 5.3 %collective-permute-start.11 = (f32[4,728,128]{2,1,0:T(8,128)S(1)}, f32[4,728,128]{2,1,0:T(8,128)}, u32[]{:S(2)}, u32[]{:S(2)}) collective-permute-start(f32[4,728,128]{2,1,0:T(8,128)S(1)} %pad_maximum_fusion.own), channel_id=1, source_target_pairs={{0,32},{32,0},{64,96},{96,64},{128,160},{160,128},{192,224},{224,1... | collective-permute-start | bytes 4472840 | tf_op jit(solution)/shard_map/ppermute | solution.py:394
  120.7 0.7 pad_add_fusion.meta
  121.4 2.4 %collective-permute-done.11.other = f32[4,728,128]{2,1,0:T(8,128)} collective-permute-done((f32[4,728,128]{2,1,0:T(8,128)S(1)}, f32[4,728,128]{2,1,0:T(8,128)}, u32[]{:S(2)}, u32[]{:S(2)}) %collective-permute-start.11) | collective-permute-done | bytes 1490976 | tf_op jit(solution)/shard_map/ppermute | solution.py:394
  123.8 47.6 %block_solve.1 = (f32[147,128]{1,0:T(8,128)}, f32[147,1024]{1,0:T(8,128)}) custom-call(s32[4]{0:T(128)} %pad_add_fusion.meta, f32[4,728,128]{2,1,0:T(8,128)} %copy-done.1, f32[4,728,128]{2,1,0:T(8,128)} %collective-permute-done.11.other, bf16[1024,1024]{1,0:T(8,128)(2,1)} %get-tuple-element.14.fh_in, bf16[1024,1024]{1,0:T(8,128)(2,1)} %get-tuple-element.15.fl_in, ...), custom_call_target="tpu_custom_call" | custom-call | tf_op jit(solution)/shard_map/block_solve/pallas_call | solution.py:397
  (24 shorter events, 1.7 us)
Async XLA Ops:
  0.6 1.5 copy-start
  2.4 12.6 %collective-permute-start.2 = (f32[448,128]{1,0:T(8,128)S(1)}, f32[448,128]{1,0:T(8,128)S(1)}, u32[]{:S(2)}, u32[]{:S(2)}) collective-permute-start(f32[448,128]{1,0:T(8,128)S(1)} %get-tuple-element.22), channel_id=1, source_target_pairs={{0,192},{32,224},{64,0},{96,32},{128,64},{160,96},{192,128},{224,1... | collective-permute-start | bytes 688136 | tf_op jit(solution)/shard_map/ppermute | solution.py:343
  5.8 9.2 %collective-permute-start.1 = (f32[448,128]{1,0:T(8,128)S(1)}, f32[448,128]{1,0:T(8,128)S(1)}, u32[]{:S(2)}, u32[]{:S(2)}) collective-permute-start(f32[448,128]{1,0:T(8,128)S(1)} %get-tuple-element.22), channel_id=1, source_target_pairs={{0,128},{32,160},{64,192},{96,224},{128,0},{160,32},{192,64},{224,... | collective-permute-start | bytes 688136 | tf_op jit(solution)/shard_map/ppermute | solution.py:343
  6.3 13.4 %collective-permute-start = (f32[448,128]{1,0:T(8,128)S(1)}, f32[448,128]{1,0:T(8,128)S(1)}, u32[]{:S(2)}, u32[]{:S(2)}) collective-permute-start(f32[448,128]{1,0:T(8,128)S(1)} %get-tuple-element.22), channel_id=1, source_target_pairs={{0,64},{32,96},{64,128},{96,160},{128,192},{160,224},{192,0},{224,... | collective-permute-start | bytes 688136 | tf_op jit(solution)/shard_map/ppermute | solution.py:343
  19.8 2.7 %copy-start.2 = (f32[4,448,128]{2,1,0:T(8,128)}, f32[4,448,128]{2,1,0:T(8,128)S(1)}, u32[]{:S(2)}) copy-start(f32[4,448,128]{2,1,0:T(8,128)S(1)} %pad_maximum_fusion.1.mine) | copy-start | bytes 2752516
  19.8 2.7 %collective-permute-start.3 = (f32[4,448,128]{2,1,0:T(8,128)S(1)}, f32[4,448,128]{2,1,0:T(8,128)S(1)}, u32[]{:S(2)}, u32[]{:S(2)}) collective-permute-start(f32[4,448,128]{2,1,0:T(8,128)S(1)} %pad_maximum_fusion.1.mine), channel_id=1, source_target_pairs={{0,32},{32,0},{64,96},{96,64},{128,160},{160,128},{192,224},{224,1... | collective-permute-start | bytes 2752520 | tf_op jit(solution)/shard_map/ppermute | solution.py:349
  22.5 1.0 copy-start.4
  38.0 3.8 %collective-permute-start.4 = (f32[2912,128]{1,0:T(8,128)}, f32[2912,128]{1,0:T(8,128)S(1)}, u32[]{:S(2)}, u32[]{:S(2)}) collective-permute-start(f32[2912,128]{1,0:T(8,128)} %get-tuple-element.13), channel_id=1, source_target_pairs={{0,32},{32,0},{64,96},{96,64},{128,160},{160,128},{192,224},{224,1... | collective-permute-start | bytes 4472840 | tf_op jit(solution)/shard_map/ppermute | solution.py:378
  41.7 1.2 copy-start.3
  45.9 11.5 %collective-permute-start.7 = (f32[728,128]{1,0:T(8,128)}, f32[728,128]{1,0:T(8,128)}, u32[]{:S(2)}, u32[]{:S(2)}) collective-permute-start(f32[728,128]{1,0:T(8,128)} %get-tuple-element.17), channel_id=1, source_target_pairs={{0,192},{32,56},{1,193},{33,57},{2,194},{34,58},{3,195},{35,59},{4... | collective-permute-start | bytes 1118216 | tf_op jit(solution)/shard_map/ppermute | solution.py:381
  48.6 8.8 %collective-permute-start.6 = (f32[728,128]{1,0:T(8,128)}, f32[728,128]{1,0:T(8,128)}, u32[]{:S(2)}, u32[]{:S(2)}) collective-permute-start(f32[728,128]{1,0:T(8,128)} %get-tuple-element.18), channel_id=1, source_target_pairs={{0,128},{32,48},{1,129},{33,49},{2,130},{34,50},{3,131},{35,51},{4... | collective-permute-start | bytes 1118216 | tf_op jit(solution)/shard_map/ppermute | solution.py:381
  49.0 11.9 %collective-permute-start.5 = (f32[728,128]{1,0:T(8,128)}, f32[728,128]{1,0:T(8,128)}, u32[]{:S(2)}, u32[]{:S(2)}) collective-permute-start(f32[728,128]{1,0:T(8,128)} %get-tuple-element.16), channel_id=1, source_target_pairs={{0,64},{32,40},{1,65},{33,41},{2,66},{34,42},{3,67},{35,43},{4,68}... | collective-permute-start | bytes 1118216 | tf_op jit(solution)/shard_map/ppermute | solution.py:381
  102.9 6.8 %collective-permute-start.10 = (f32[728,128]{1,0:T(8,128)S(1)}, f32[728,128]{1,0:T(8,128)S(1)}, u32[]{:S(2)}, u32[]{:S(2)}) collective-permute-start(f32[728,128]{1,0:T(8,128)S(1)} %get-tuple-element.20), channel_id=1, source_target_pairs={{0,192},{32,56},{1,193},{33,57},{2,194},{34,58},{3,195},{35,59},{4... | collective-permute-start | bytes 1118216 | tf_op jit(solution)/shard_map/ppermute | solution.py:393
  103.0 8.1 %collective-permute-start.9 = (f32[728,128]{1,0:T(8,128)S(1)}, f32[728,128]{1,0:T(8,128)S(1)}, u32[]{:S(2)}, u32[]{:S(2)}) collective-permute-start(f32[728,128]{1,0:T(8,128)S(1)} %get-tuple-element.20), channel_id=1, source_target_pairs={{0,128},{32,48},{1,129},{33,49},{2,130},{34,50},{3,131},{35,51},{4... | collective-permute-start | bytes 1118216 | tf_op jit(solution)/shard_map/ppermute | solution.py:393
  103.1 12.2 %collective-permute-start.8 = (f32[728,128]{1,0:T(8,128)S(1)}, f32[728,128]{1,0:T(8,128)S(1)}, u32[]{:S(2)}, u32[]{:S(2)}) collective-permute-start(f32[728,128]{1,0:T(8,128)S(1)} %get-tuple-element.20), channel_id=1, source_target_pairs={{0,64},{32,40},{1,65},{33,41},{2,66},{34,42},{3,67},{35,43},{4,68}... | collective-permute-start | bytes 1118216 | tf_op jit(solution)/shard_map/ppermute | solution.py:393
  115.4 8.3 %copy-start.1 = (f32[4,728,128]{2,1,0:T(8,128)}, f32[4,728,128]{2,1,0:T(8,128)S(1)}, u32[]{:S(2)}) copy-start(f32[4,728,128]{2,1,0:T(8,128)S(1)} %pad_maximum_fusion.own) | copy-start | bytes 4472836
  115.4 8.3 %collective-permute-start.11 = (f32[4,728,128]{2,1,0:T(8,128)S(1)}, f32[4,728,128]{2,1,0:T(8,128)}, u32[]{:S(2)}, u32[]{:S(2)}) collective-permute-start(f32[4,728,128]{2,1,0:T(8,128)S(1)} %pad_maximum_fusion.own), channel_id=1, source_target_pairs={{0,32},{32,0},{64,96},{96,64},{128,160},{160,128},{192,224},{224,1... | collective-permute-start | bytes 4472840 | tf_op jit(solution)/shard_map/ppermute | solution.py:394

commit v2 on v1

--- a/solution.py
+++ b/solution.py
@@ -4,6 +4,7 @@
 from jax.experimental import pallas as pl
 from jax.experimental.pallas import tpu as pltpu
 from jax.sharding import PartitionSpec as P
+
 
 ridge_weight = 0.05
 D = 440
@@ -230,6 +231,7 @@
         ridge_weight,
         0.0,
     )
+
     def panel(k, carry):
         o = pl.multiple_of(k * (FB + PAD) - 64 * k * (k - 1), 8)
         dinv[...] = p[pl.ds(o, 128), :] + eye
@@ -325,6 +327,13 @@
 core_swap = [(f, f ^ 1) for f in range(8)]
 
 
+def shifted(perm, axis, values):
+    got = {}
+    for s in (2, 1, 3):
+        got[s] = lax.ppermute(values[s], axis, perm(s))
+    return [got[s] for s in (1, 2, 3)]
+
+
 def per_device(samples, residual, bank, bank_phase, bank_weights, block_index):
     chosen = block_index[0]
     feat = lax.axis_index("feat")
@@ -340,7 +349,7 @@
         axis=0,
     )
     local_weights = lax.dynamic_index_in_dim(bank_weights, chosen, 0, keepdims=False)
-    mine = jnp.stack([block] + [lax.ppermute(block, "feat", x_perm(s)) for s in (1, 2, 3)])
+    mine = jnp.stack([block] + shifted(x_perm, "feat", [block] * 4))
     order = [
         (x + 4 - f // 2) % 4 + jnp.where(core == f % 2, 0, 4) for f in range(8)
     ]
@@ -377,20 +386,18 @@
     spot = jnp.where(core == 0, x, y)
     half = keep + lax.ppermute(give, "feat", core_swap)
     quarters = half.reshape(4, QUART, 128)
-    got = [
-        lax.ppermute(
-            lax.dynamic_index_in_dim(quarters, (spot + s) % 4, 0, keepdims=False), BOTH, ring_perm(s)
-        )
-        for s in (1, 2, 3)
-    ]
-    quarter = lax.dynamic_index_in_dim(quarters, spot, 0, keepdims=False) + got[0] + got[1] + got[2]
+    leaving = [
+        lax.dynamic_index_in_dim(quarters, (spot + s) % 4, 0, keepdims=False) for s in range(4)
+    ]
+    got = shifted(ring_perm, BOTH, leaving)
+    quarter = leaving[0] + got[0] + got[1] + got[2]
     spread = jnp.pad(quarter, ((0, 32 * CHUNK - QUART), (0, 0))).reshape(32, CHUNK, 128)
     chunk = jnp.sum(lax.all_to_all(spread, BOTH, 0, 0, axis_index_groups=GROUPS), axis=0)
     full = lax.all_to_all(
         jnp.broadcast_to(chunk[None], (32, CHUNK, 128)), BOTH, 0, 0, axis_index_groups=GROUPS
     )
     quarter = full.reshape(32 * CHUNK, 128)[:QUART]
-    own = jnp.stack([quarter] + [lax.ppermute(quarter, BOTH, ring_perm(s)) for s in (1, 2, 3)])
+    own = jnp.stack([quarter] + shifted(ring_perm, BOTH, [quarter] * 4))
     other = lax.ppermute(own, "feat", core_swap)
 
     where = jnp.stack([feat, core, spot, jnp.where(core == 0, y, x)]).astype(jnp.int32)

time: 172 us -> 172 us (level)
  no operation moved by 1% of the time
where the time goes in v2:
time: 172 us
  Pallas kernels  62.1 us (36%)
  blocking collectives  40.6 us (24%)
  waiting for transfers between devices  40 us (23%)
  starting transfers between devices  16.3 us (9%)
  local copies, waits for them, and re-layouts  6.55 us (4%)
  other arithmetic  4.3 us (2%)
    pallas_call x1, Pallas kernels, per_device(): pl.pallas_call(solve_kernel, out_shape=(jax.ShapeDtypeStruct((C, 128), f3...  47.6 us
    ppermute x9, waiting for transfers between devices, shifted(): got[s] = lax.ppermute(values[s], axis, perm(s))  32.4 us
    all_to_all x1, blocking collectives, per_device(): lax.all_to_all(spread, BOTH, 0, 0, axis_index_groups=GROUPS)  21.8 us
    all_to_all x1, blocking collectives, per_device(): lax.all_to_all(jnp.broadcast_to(chunk[None], (32, CHUNK, 128)), BOTH, 0,...  18.8 us
    pallas_call x1, Pallas kernels, per_device(): pl.pallas_call(gram_kernel, out_shape=(jax.ShapeDtypeStruct((HALF, 128),...  14.5 us
    ppermute x9, starting transfers between devices, shifted(): got[s] = lax.ppermute(values[s], axis, perm(s))  9.8 us
    ppermute x1, starting transfers between devices, per_device(): other = lax.ppermute(own, 'feat', core_swap)  5.28 us
  transfers between devices with their start and end apart: 12, of which 10 were waited for; matrix products, arithmetic and copies ran while one was open for 2% of the time, Pallas kernels for 0%

profile of v2, /device:TPU:1, one launch (start us, length us, event | category | flops | bytes accessed | tf_op | source)
XLA Modules:
  0.0 171.5 jit_solution(3363693653189180576)
XLA Ops:
  1.4 0.7 constant_dynamic-slice_fusion.1
  2.4 3.4 %collective-permute-start.2 = (f32[448,128]{1,0:T(8,128)S(1)}, f32[448,128]{1,0:T(8,128)S(1)}, u32[]{:S(2)}, u32[]{:S(2)}) collective-permute-start(f32[448,128]{1,0:T(8,128)S(1)} %get-tuple-element.22), channel_id=1, source_target_pairs={{0,192},{32,224},{64,0},{96,32},{128,64},{160,96},{192,128},{224,1... | collective-permute-start | bytes 688136 | tf_op jit(solution)/shard_map/ppermute | solution.py:333
  6.3 0.6 collective-permute-start
  6.9 1.1 constant_dynamic-slice_fusion
  8.0 0.6 copy.11
  8.6 0.7 stack.95.meta
  9.3 5.6 %collective-permute-done.2 = f32[448,128]{1,0:T(8,128)S(1)} collective-permute-done((f32[448,128]{1,0:T(8,128)S(1)}, f32[448,128]{1,0:T(8,128)S(1)}, u32[]{:S(2)}, u32[]{:S(2)}) %collective-permute-start.2) | collective-permute-done | bytes 229408 | tf_op jit(solution)/shard_map/ppermute | solution.py:333
  14.9 4.8 %collective-permute-done = f32[448,128]{1,0:T(8,128)S(1)} collective-permute-done((f32[448,128]{1,0:T(8,128)S(1)}, f32[448,128]{1,0:T(8,128)S(1)}, u32[]{:S(2)}, u32[]{:S(2)}) %collective-permute-start) | collective-permute-done | bytes 229408 | tf_op jit(solution)/shard_map/ppermute | solution.py:333
  19.8 0.6 collective-permute-start.3
  20.4 2.1 %collective-permute-done.3.theirs = f32[4,448,128]{2,1,0:T(8,128)S(1)} collective-permute-done((f32[4,448,128]{2,1,0:T(8,128)S(1)}, f32[4,448,128]{2,1,0:T(8,128)S(1)}, u32[]{:S(2)}, u32[]{:S(2)}) %collective-permute-start.3) | collective-permute-done | bytes 917536 | tf_op jit(solution)/shard_map/ppermute | solution.py:358
  22.5 1.0 copy-done.4
  23.5 14.5 %features_gram.1 = (f32[2912,128]{1,0:T(8,128)}, f32[2912,128]{1,0:T(8,128)}, bf16[1024,1024]{1,0:T(8,128)(2,1)}, bf16[1024,1024]{1,0:T(8,128)(2,1)}) custom-call(s32[10]{0:T(128)} %stack.95.meta, f32[4,448,128]{2,1,0:T(8,128)} %copy-done.2, f32[4,448,128]{2,1,0:T(8,128)} %copy-done.4, f32[440,1024]{1,0:T(8,128)} %samples_in.1, f32[147,1024]{1,0:T(8,128)} %residual.1, ...), custom_call_target="tpu_custom_call" | custom-call | tf_op jit(solution)/shard_map/features_gram/pallas_call | solution.py:362
  38.0 0.6 collective-permute-start.4
  38.6 3.1 %collective-permute-done.4 = f32[2912,128]{1,0:T(8,128)S(1)} collective-permute-done((f32[2912,128]{1,0:T(8,128)}, f32[2912,128]{1,0:T(8,128)S(1)}, u32[]{:S(2)}, u32[]{:S(2)}) %collective-permute-start.4) | collective-permute-done | bytes 1490976 | tf_op jit(solution)/shard_map/ppermute | solution.py:387
  41.7 1.2 copy-done.3
  42.9 2.0 %add.136 = f32[2912,128]{1,0:T(8,128)S(1)} add(f32[2912,128]{1,0:T(8,128)} %get-tuple-element.12, f32[2912,128]{1,0:T(8,128)} %copy-done.3) | non-fusion elementwise | flops 372736 | bytes 4472832 | tf_op jit(solution)/shard_map/add | solution.py:387
  44.9 1.0 dynamic-slice_bitcast_fusion.2
  45.9 2.7 %collective-permute-start.7 = (f32[728,128]{1,0:T(8,128)}, f32[728,128]{1,0:T(8,128)}, u32[]{:S(2)}, u32[]{:S(2)}) collective-permute-start(f32[728,128]{1,0:T(8,128)} %get-tuple-element.17), channel_id=1, source_target_pairs={{0,192},{32,56},{1,193},{33,57},{2,194},{34,58},{3,195},{35,59},{4... | collective-permute-start | bytes 1118216 | tf_op jit(solution)/shard_map/ppermute | solution.py:333
  49.0 0.7 collective-permute-start.5
  49.7 7.8 %collective-permute-done.7 = f32[728,128]{1,0:T(8,128)} collective-permute-done((f32[728,128]{1,0:T(8,128)}, f32[728,128]{1,0:T(8,128)}, u32[]{:S(2)}, u32[]{:S(2)}) %collective-permute-start.7) | collective-permute-done | bytes 372768 | tf_op jit(solution)/shard_map/ppermute | solution.py:333
  57.5 3.4 %collective-permute-done.5 = f32[728,128]{1,0:T(8,128)} collective-permute-done((f32[728,128]{1,0:T(8,128)}, f32[728,128]{1,0:T(8,128)}, u32[]{:S(2)}, u32[]{:S(2)}) %collective-permute-start.5) | collective-permute-done | bytes 372768 | tf_op jit(solution)/shard_map/ppermute | solution.py:333
  60.9 1.3 fusion.1
  62.2 21.8 %all_to_all.10 = f32[32,24,128]{2,1,0:T(8,128)S(1)} all-to-all(f32[32,24,128]{2,1,0:T(8,128)S(1)} %bitcast.49), channel_id=1, replica_groups={{0,1,2,3,4,5,6,7,8,9,10,11,12,13,14,15,16,17,18,19,20,21,22,23,24,25,26..., dimensions={0} | all-to-all | bytes 786432 | tf_op jit(solution)/shard_map/all_to_all | solution.py:395
  84.0 18.8 %all_to_all.11 = f32[32,24,128]{2,1,0:T(8,128)S(1)} all-to-all(f32[32,24,128]{2,1,0:T(8,128)S(1)} %broadcast_in_dim.10), channel_id=1, replica_groups={{0,1,2,3,4,5,6,7,8,9,10,11,12,13,14,15,16,17,18,19,20,21,22,23,24,25,26..., dimensions={0} | all-to-all | bytes 786432 | tf_op jit(solution)/shard_map/all_to_all | solution.py:396
  103.1 1.4 collective-permute-start.8
  104.4 5.2 %collective-permute-done.10 = f32[728,128]{1,0:T(8,128)S(1)} collective-permute-done((f32[728,128]{1,0:T(8,128)S(1)}, f32[728,128]{1,0:T(8,128)S(1)}, u32[]{:S(2)}, u32[]{:S(2)}) %collective-permute-start.10) | collective-permute-done | bytes 372768 | tf_op jit(solution)/shard_map/ppermute | solution.py:333
  109.7 1.4 collective-permute-done.9
  111.1 4.2 %collective-permute-done.8 = f32[728,128]{1,0:T(8,128)S(1)} collective-permute-done((f32[728,128]{1,0:T(8,128)S(1)}, f32[728,128]{1,0:T(8,128)S(1)}, u32[]{:S(2)}, u32[]{:S(2)}) %collective-permute-start.8) | collective-permute-done | bytes 372768 | tf_op jit(solution)/shard_map/ppermute | solution.py:333
  115.4 5.3 %collective-permute-start.11 = (f32[4,728,128]{2,1,0:T(8,128)S(1)}, f32[4,728,128]{2,1,0:T(8,128)}, u32[]{:S(2)}, u32[]{:S(2)}) collective-permute-start(f32[4,728,128]{2,1,0:T(8,128)S(1)} %pad_maximum_fusion.own), channel_id=1, source_target_pairs={{0,32},{32,0},{64,96},{96,64},{128,160},{160,128},{192,224},{224,1... | collective-permute-start | bytes 4472840 | tf_op jit(solution)/shard_map/ppermute | solution.py:401
  120.7 0.7 pad_add_fusion.meta
  121.4 2.4 %collective-permute-done.11.other = f32[4,728,128]{2,1,0:T(8,128)} collective-permute-done((f32[4,728,128]{2,1,0:T(8,128)S(1)}, f32[4,728,128]{2,1,0:T(8,128)}, u32[]{:S(2)}, u32[]{:S(2)}) %collective-permute-start.11) | collective-permute-done | bytes 1490976 | tf_op jit(solution)/shard_map/ppermute | solution.py:401
  123.8 47.6 %block_solve.1 = (f32[147,128]{1,0:T(8,128)}, f32[147,1024]{1,0:T(8,128)}) custom-call(s32[4]{0:T(128)} %pad_add_fusion.meta, f32[4,728,128]{2,1,0:T(8,128)} %copy-done.1, f32[4,728,128]{2,1,0:T(8,128)} %collective-permute-done.11.other, bf16[1024,1024]{1,0:T(8,128)(2,1)} %get-tuple-element.14.fh_in, bf16[1024,1024]{1,0:T(8,128)(2,1)} %get-tuple-element.15.fl_in, ...), custom_call_target="tpu_custom_call" | custom-call | tf_op jit(solution)/shard_map/block_solve/pallas_call | solution.py:404
  (24 shorter events, 1.7 us)
Async XLA Ops:
  0.6 1.5 copy-start
  2.4 12.6 %collective-permute-start.2 = (f32[448,128]{1,0:T(8,128)S(1)}, f32[448,128]{1,0:T(8,128)S(1)}, u32[]{:S(2)}, u32[]{:S(2)}) collective-permute-start(f32[448,128]{1,0:T(8,128)S(1)} %get-tuple-element.22), channel_id=1, source_target_pairs={{0,192},{32,224},{64,0},{96,32},{128,64},{160,96},{192,128},{224,1... | collective-permute-start | bytes 688136 | tf_op jit(solution)/shard_map/ppermute | solution.py:333
  5.8 9.2 %collective-permute-start.1 = (f32[448,128]{1,0:T(8,128)S(1)}, f32[448,128]{1,0:T(8,128)S(1)}, u32[]{:S(2)}, u32[]{:S(2)}) collective-permute-start(f32[448,128]{1,0:T(8,128)S(1)} %get-tuple-element.22), channel_id=1, source_target_pairs={{0,128},{32,160},{64,192},{96,224},{128,0},{160,32},{192,64},{224,... | collective-permute-start | bytes 688136 | tf_op jit(solution)/shard_map/ppermute | solution.py:333
  6.3 13.4 %collective-permute-start = (f32[448,128]{1,0:T(8,128)S(1)}, f32[448,128]{1,0:T(8,128)S(1)}, u32[]{:S(2)}, u32[]{:S(2)}) collective-permute-start(f32[448,128]{1,0:T(8,128)S(1)} %get-tuple-element.22), channel_id=1, source_target_pairs={{0,64},{32,96},{64,128},{96,160},{128,192},{160,224},{192,0},{224,... | collective-permute-start | bytes 688136 | tf_op jit(solution)/shard_map/ppermute | solution.py:333
  19.8 2.7 %copy-start.2 = (f32[4,448,128]{2,1,0:T(8,128)}, f32[4,448,128]{2,1,0:T(8,128)S(1)}, u32[]{:S(2)}) copy-start(f32[4,448,128]{2,1,0:T(8,128)S(1)} %pad_maximum_fusion.1.mine) | copy-start | bytes 2752516
  19.8 2.7 %collective-permute-start.3 = (f32[4,448,128]{2,1,0:T(8,128)S(1)}, f32[4,448,128]{2,1,0:T(8,128)S(1)}, u32[]{:S(2)}, u32[]{:S(2)}) collective-permute-start(f32[4,448,128]{2,1,0:T(8,128)S(1)} %pad_maximum_fusion.1.mine), channel_id=1, source_target_pairs={{0,32},{32,0},{64,96},{96,64},{128,160},{160,128},{192,224},{224,1... | collective-permute-start | bytes 2752520 | tf_op jit(solution)/shard_map/ppermute | solution.py:358
  22.5 1.0 copy-start.4
  38.0 3.8 %collective-permute-start.4 = (f32[2912,128]{1,0:T(8,128)}, f32[2912,128]{1,0:T(8,128)S(1)}, u32[]{:S(2)}, u32[]{:S(2)}) collective-permute-start(f32[2912,128]{1,0:T(8,128)} %get-tuple-element.13), channel_id=1, source_target_pairs={{0,32},{32,0},{64,96},{96,64},{128,160},{160,128},{192,224},{224,1... | collective-permute-start | bytes 4472840 | tf_op jit(solution)/shard_map/ppermute | solution.py:387
  41.7 1.2 copy-start.3
  45.9 11.5 %collective-permute-start.7 = (f32[728,128]{1,0:T(8,128)}, f32[728,128]{1,0:T(8,128)}, u32[]{:S(2)}, u32[]{:S(2)}) collective-permute-start(f32[728,128]{1,0:T(8,128)} %get-tuple-element.17), channel_id=1, source_target_pairs={{0,192},{32,56},{1,193},{33,57},{2,194},{34,58},{3,195},{35,59},{4... | collective-permute-start | bytes 1118216 | tf_op jit(solution)/shard_map/ppermute | solution.py:333
  48.6 8.8 %collective-permute-start.6 = (f32[728,128]{1,0:T(8,128)}, f32[728,128]{1,0:T(8,128)}, u32[]{:S(2)}, u32[]{:S(2)}) collective-permute-start(f32[728,128]{1,0:T(8,128)} %get-tuple-element.18), channel_id=1, source_target_pairs={{0,128},{32,48},{1,129},{33,49},{2,130},{34,50},{3,131},{35,51},{4... | collective-permute-start | bytes 1118216 | tf_op jit(solution)/shard_map/ppermute | solution.py:333
  49.0 11.9 %collective-permute-start.5 = (f32[728,128]{1,0:T(8,128)}, f32[728,128]{1,0:T(8,128)}, u32[]{:S(2)}, u32[]{:S(2)}) collective-permute-start(f32[728,128]{1,0:T(8,128)} %get-tuple-element.16), channel_id=1, source_target_pairs={{0,64},{32,40},{1,65},{33,41},{2,66},{34,42},{3,67},{35,43},{4,68}... | collective-permute-start | bytes 1118216 | tf_op jit(solution)/shard_map/ppermute | solution.py:333
  102.9 6.8 %collective-permute-start.10 = (f32[728,128]{1,0:T(8,128)S(1)}, f32[728,128]{1,0:T(8,128)S(1)}, u32[]{:S(2)}, u32[]{:S(2)}) collective-permute-start(f32[728,128]{1,0:T(8,128)S(1)} %get-tuple-element.20), channel_id=1, source_target_pairs={{0,192},{32,56},{1,193},{33,57},{2,194},{34,58},{3,195},{35,59},{4... | collective-permute-start | bytes 1118216 | tf_op jit(solution)/shard_map/ppermute | solution.py:333
  103.0 8.1 %collective-permute-start.9 = (f32[728,128]{1,0:T(8,128)S(1)}, f32[728,128]{1,0:T(8,128)S(1)}, u32[]{:S(2)}, u32[]{:S(2)}) collective-permute-start(f32[728,128]{1,0:T(8,128)S(1)} %get-tuple-element.20), channel_id=1, source_target_pairs={{0,128},{32,48},{1,129},{33,49},{2,130},{34,50},{3,131},{35,51},{4... | collective-permute-start | bytes 1118216 | tf_op jit(solution)/shard_map/ppermute | solution.py:333
  103.1 12.2 %collective-permute-start.8 = (f32[728,128]{1,0:T(8,128)S(1)}, f32[728,128]{1,0:T(8,128)S(1)}, u32[]{:S(2)}, u32[]{:S(2)}) collective-permute-start(f32[728,128]{1,0:T(8,128)S(1)} %get-tuple-element.20), channel_id=1, source_target_pairs={{0,64},{32,40},{1,65},{33,41},{2,66},{34,42},{3,67},{35,43},{4,68}... | collective-permute-start | bytes 1118216 | tf_op jit(solution)/shard_map/ppermute | solution.py:333
  115.4 8.3 %copy-start.1 = (f32[4,728,128]{2,1,0:T(8,128)}, f32[4,728,128]{2,1,0:T(8,128)S(1)}, u32[]{:S(2)}) copy-start(f32[4,728,128]{2,1,0:T(8,128)S(1)} %pad_maximum_fusion.own) | copy-start | bytes 4472836
  115.4 8.3 %collective-permute-start.11 = (f32[4,728,128]{2,1,0:T(8,128)S(1)}, f32[4,728,128]{2,1,0:T(8,128)}, u32[]{:S(2)}, u32[]{:S(2)}) collective-permute-start(f32[4,728,128]{2,1,0:T(8,128)S(1)} %pad_maximum_fusion.own), channel_id=1, source_target_pairs={{0,32},{32,0},{64,96},{96,64},{128,160},{160,128},{192,224},{224,1... | collective-permute-start | bytes 4472840 | tf_op jit(solution)/shard_map/ppermute | solution.py:401

commit v3 on v2

--- a/solution.py
+++ b/solution.py
@@ -205,11 +205,6 @@
     return jnp.concatenate([a, a, b, a, c, b], axis=1)
 
 
-def stack_right(x):
-    a, b, c = split3(x)
-    return jnp.concatenate([a, b, a, c, a, b], axis=1)
-
-
 def solve_kernel(meta, own, other, fh_in, fl_in, residual, weights, new_weights, new_residual, p, dinv, us, fh, fl, sem, fsem):
     core = meta[1]
     pieces = []
@@ -258,15 +253,15 @@
         gain = gain[:, :128] + gain[:, 128:]
         if k < NB - 1:
             left = stack_left(gain)
-            right = stack_right(below[: m - PAD])
+            right = jnp.concatenate([a, b, a, c, a, b], axis=1)[: m - PAD]
             j = k + 1
             if (NB - j) % 2:
                 p[OFF[j] : OFF[j] + m, :] = p[OFF[j] : OFF[j] + m, :] - dot(left, right[:128], NT)
                 j += 1
             while j < NB:
-                b = (j - k - 1) * 128
-                n = m - b
-                both = dot(left[b:], right[b : b + 256], NT)
+                skip = (j - k - 1) * 128
+                n = m - skip
+                both = dot(left[skip:], right[skip : skip + 256], NT)
                 p[OFF[j] : OFF[j] + n, :] = p[OFF[j] : OFF[j] + n, :] - both[:, :128]
                 n -= 128
                 p[OFF[j + 1] : OFF[j + 1] + n, :] = p[OFF[j + 1] : OFF[j + 1] + n, :] - both[128:, 128:]
@@ -384,11 +379,15 @@
     )(meta, mine, theirs, samples, residual, local_weights)
 
     spot = jnp.where(core == 0, x, y)
-    half = keep + lax.ppermute(give, "feat", core_swap)
-    quarters = half.reshape(4, QUART, 128)
-    leaving = [
-        lax.dynamic_index_in_dim(quarters, (spot + s) % 4, 0, keepdims=False) for s in range(4)
-    ]
+    received = lax.ppermute(give, "feat", core_swap)
+
+    def leaving_quarter(s):
+        at = (spot + s) % 4
+        return lax.dynamic_index_in_dim(
+            keep.reshape(4, QUART, 128), at, 0, keepdims=False
+        ) + lax.dynamic_index_in_dim(received.reshape(4, QUART, 128), at, 0, keepdims=False)
+
+    leaving = [leaving_quarter(s) for s in range(4)]
     got = shifted(ring_perm, BOTH, leaving)
     quarter = leaving[0] + got[0] + got[1] + got[2]
     spread = jnp.pad(quarter, ((0, 32 * CHUNK - QUART), (0, 0))).reshape(32, CHUNK, 128)

time: 172 us -> 170 us (0.988)
  local copies, waits for them, and re-layouts: 6.55 us -> 4.36 us
where the time goes in v3:
time: 170 us
  Pallas kernels  62.1 us (37%)
  blocking collectives  40.6 us (24%)
  waiting for transfers between devices  40 us (24%)
  starting transfers between devices  16.3 us (10%)
  other arithmetic  4.7 us (3%)
  local copies, waits for them, and re-layouts  4.36 us (3%)
  between operations  1.71 us (1%)
    pallas_call x1, Pallas kernels, per_device(): pl.pallas_call(solve_kernel, out_shape=(jax.ShapeDtypeStruct((C, 128), f3...  47.6 us
    ppermute x9, waiting for transfers between devices, shifted(): got[s] = lax.ppermute(values[s], axis, perm(s))  32.4 us
    all_to_all x1, blocking collectives, per_device(): lax.all_to_all(spread, BOTH, 0, 0, axis_index_groups=GROUPS)  21.8 us
    all_to_all x1, blocking collectives, per_device(): lax.all_to_all(jnp.broadcast_to(chunk[None], (32, CHUNK, 128)), BOTH, 0,...  18.8 us
    pallas_call x1, Pallas kernels, per_device(): pl.pallas_call(gram_kernel, out_shape=(jax.ShapeDtypeStruct((HALF, 128),...  14.5 us
    ppermute x9, starting transfers between devices, shifted(): got[s] = lax.ppermute(values[s], axis, perm(s))  9.82 us
    ppermute x1, starting transfers between devices, per_device(): other = lax.ppermute(own, 'feat', core_swap)  5.27 us
  transfers between devices with their start and end apart: 12, of which 10 were waited for; matrix products, arithmetic and copies ran while one was open for 2% of the time, Pallas kernels for 0%

profile of v3, /device:TPU:1, one launch (start us, length us, event | category | flops | bytes accessed | tf_op | source)
XLA Modules:
  0.0 169.7 jit_solution(18132565779444536920)
XLA Ops:
  1.4 0.7 constant_dynamic-slice_fusion.1
  2.4 3.4 %collective-permute-start.2 = (f32[448,128]{1,0:T(8,128)S(1)}, f32[448,128]{1,0:T(8,128)S(1)}, u32[]{:S(2)}, u32[]{:S(2)}) collective-permute-start(f32[448,128]{1,0:T(8,128)S(1)} %get-tuple-element.22), channel_id=1, source_target_pairs={{0,192},{32,224},{64,0},{96,32},{128,64},{160,96},{192,128},{224,1... | collective-permute-start | bytes 688136 | tf_op jit(solution)/shard_map/ppermute | solution.py:328
  5.8 0.5 collective-permute-start.1
  6.3 0.6 collective-permute-start
  6.9 1.1 constant_dynamic-slice_fusion
  8.0 0.6 copy.11
  8.6 0.7 stack.95.meta
  9.3 5.6 %collective-permute-done.2 = f32[448,128]{1,0:T(8,128)S(1)} collective-permute-done((f32[448,128]{1,0:T(8,128)S(1)}, f32[448,128]{1,0:T(8,128)S(1)}, u32[]{:S(2)}, u32[]{:S(2)}) %collective-permute-start.2) | collective-permute-done | bytes 229408 | tf_op jit(solution)/shard_map/ppermute | solution.py:328
  14.9 4.8 %collective-permute-done = f32[448,128]{1,0:T(8,128)S(1)} collective-permute-done((f32[448,128]{1,0:T(8,128)S(1)}, f32[448,128]{1,0:T(8,128)S(1)}, u32[]{:S(2)}, u32[]{:S(2)}) %collective-permute-start) | collective-permute-done | bytes 229408 | tf_op jit(solution)/shard_map/ppermute | solution.py:328
  19.8 0.6 collective-permute-start.3
  20.4 2.1 %collective-permute-done.3.theirs = f32[4,448,128]{2,1,0:T(8,128)S(1)} collective-permute-done((f32[4,448,128]{2,1,0:T(8,128)S(1)}, f32[4,448,128]{2,1,0:T(8,128)S(1)}, u32[]{:S(2)}, u32[]{:S(2)}) %collective-permute-start.3) | collective-permute-done | bytes 917536 | tf_op jit(solution)/shard_map/ppermute | solution.py:353
  22.5 1.0 copy-done.3
  23.5 14.5 %features_gram.1 = (f32[2912,128]{1,0:T(8,128)}, f32[2912,128]{1,0:T(8,128)}, bf16[1024,1024]{1,0:T(8,128)(2,1)}, bf16[1024,1024]{1,0:T(8,128)(2,1)}) custom-call(s32[10]{0:T(128)} %stack.95.meta, f32[4,448,128]{2,1,0:T(8,128)} %copy-done.2, f32[4,448,128]{2,1,0:T(8,128)} %copy-done.3, f32[440,1024]{1,0:T(8,128)} %samples_in.1, f32[147,1024]{1,0:T(8,128)} %residual.1, ...), custom_call_target="tpu_custom_call" | custom-call | tf_op jit(solution)/shard_map/features_gram/pallas_call | solution.py:357
  37.9 0.6 collective-permute-start.4
  38.6 3.1 %collective-permute-done.4 = f32[2912,128]{1,0:T(8,128)S(1)} collective-permute-done((f32[2912,128]{1,0:T(8,128)}, f32[2912,128]{1,0:T(8,128)S(1)}, u32[]{:S(2)}, u32[]{:S(2)}) %collective-permute-start.4) | collective-permute-done | bytes 1490976 | tf_op jit(solution)/shard_map/ppermute | solution.py:382
  41.7 2.2 %add_bitcast_fusion.2 = (f32[728,128]{1,0:T(8,128)}, f32[728,128]{1,0:T(8,128)}, f32[728,128]{1,0:T(8,128)}) fusion(f32[4,728,128]{2,1,0:T(8,128)S(1)} %bitcast.52, s32[]{:T(128)S(6)} %select_n.118, f32[4,728,128]{2,1,0:T(8,128)} %bitcast.50, s32[]{:T(128)S(6)} %select_n.122, s32[]{:T(128)S(6)} %select_n.120), kind=kLoop, calls=%fused_computation.7 | loop fusion | flops 279552 | bytes 3354636 | tf_op jit(solution)/shard_map/add | solution.py:386
  44.0 2.7 %collective-permute-start.7 = (f32[728,128]{1,0:T(8,128)}, f32[728,128]{1,0:T(8,128)}, u32[]{:S(2)}, u32[]{:S(2)}) collective-permute-start(f32[728,128]{1,0:T(8,128)} %get-tuple-element.17), channel_id=1, source_target_pairs={{0,192},{32,56},{1,193},{33,57},{2,194},{34,58},{3,195},{35,59},{4... | collective-permute-start | bytes 1118216 | tf_op jit(solution)/shard_map/ppermute | solution.py:328
  46.7 0.3 collective-permute-start.6
  47.0 0.7 collective-permute-start.5
  47.7 7.8 %collective-permute-done.7 = f32[728,128]{1,0:T(8,128)} collective-permute-done((f32[728,128]{1,0:T(8,128)}, f32[728,128]{1,0:T(8,128)}, u32[]{:S(2)}, u32[]{:S(2)}) %collective-permute-start.7) | collective-permute-done | bytes 372768 | tf_op jit(solution)/shard_map/ppermute | solution.py:328
  55.5 3.4 %collective-permute-done.5 = f32[728,128]{1,0:T(8,128)} collective-permute-done((f32[728,128]{1,0:T(8,128)}, f32[728,128]{1,0:T(8,128)}, u32[]{:S(2)}, u32[]{:S(2)}) %collective-permute-start.5) | collective-permute-done | bytes 372768 | tf_op jit(solution)/shard_map/ppermute | solution.py:328
  58.9 1.4 fusion.1
  60.4 21.8 %all_to_all.10 = f32[32,24,128]{2,1,0:T(8,128)S(1)} all-to-all(f32[32,24,128]{2,1,0:T(8,128)S(1)} %bitcast.48), channel_id=1, replica_groups={{0,1,2,3,4,5,6,7,8,9,10,11,12,13,14,15,16,17,18,19,20,21,22,23,24,25,26..., dimensions={0} | all-to-all | bytes 786432 | tf_op jit(solution)/shard_map/all_to_all | solution.py:394
  82.3 18.8 %all_to_all.11 = f32[32,24,128]{2,1,0:T(8,128)S(1)} all-to-all(f32[32,24,128]{2,1,0:T(8,128)S(1)} %broadcast_in_dim.10), channel_id=1, replica_groups={{0,1,2,3,4,5,6,7,8,9,10,11,12,13,14,15,16,17,18,19,20,21,22,23,24,25,26..., dimensions={0} | all-to-all | bytes 786432 | tf_op jit(solution)/shard_map/all_to_all | solution.py:395
  101.3 1.4 collective-permute-start.8
  102.6 5.2 %collective-permute-done.10 = f32[728,128]{1,0:T(8,128)S(1)} collective-permute-done((f32[728,128]{1,0:T(8,128)S(1)}, f32[728,128]{1,0:T(8,128)S(1)}, u32[]{:S(2)}, u32[]{:S(2)}) %collective-permute-start.10) | collective-permute-done | bytes 372768 | tf_op jit(solution)/shard_map/ppermute | solution.py:328
  107.8 1.4 collective-permute-done.9
  109.2 4.2 %collective-permute-done.8 = f32[728,128]{1,0:T(8,128)S(1)} collective-permute-done((f32[728,128]{1,0:T(8,128)S(1)}, f32[728,128]{1,0:T(8,128)S(1)}, u32[]{:S(2)}, u32[]{:S(2)}) %collective-permute-start.8) | collective-permute-done | bytes 372768 | tf_op jit(solution)/shard_map/ppermute | solution.py:328
  113.6 5.3 %collective-permute-start.11 = (f32[4,728,128]{2,1,0:T(8,128)S(1)}, f32[4,728,128]{2,1,0:T(8,128)}, u32[]{:S(2)}, u32[]{:S(2)}) collective-permute-start(f32[4,728,128]{2,1,0:T(8,128)S(1)} %pad_maximum_fusion.own), channel_id=1, source_target_pairs={{0,32},{32,0},{64,96},{96,64},{128,160},{160,128},{192,224},{224,1... | collective-permute-start | bytes 4472840 | tf_op jit(solution)/shard_map/ppermute | solution.py:400
  118.9 0.7 pad_add_fusion.meta
  119.5 2.4 %collective-permute-done.11.other = f32[4,728,128]{2,1,0:T(8,128)} collective-permute-done((f32[4,728,128]{2,1,0:T(8,128)S(1)}, f32[4,728,128]{2,1,0:T(8,128)}, u32[]{:S(2)}, u32[]{:S(2)}) %collective-permute-start.11) | collective-permute-done | bytes 1490976 | tf_op jit(solution)/shard_map/ppermute | solution.py:400
  121.9 47.6 %block_solve.1 = (f32[147,128]{1,0:T(8,128)}, f32[147,1024]{1,0:T(8,128)}) custom-call(s32[4]{0:T(128)} %pad_add_fusion.meta, f32[4,728,128]{2,1,0:T(8,128)} %copy-done.1, f32[4,728,128]{2,1,0:T(8,128)} %collective-permute-done.11.other, bf16[1024,1024]{1,0:T(8,128)(2,1)} %get-tuple-element.14.fh_in, bf16[1024,1024]{1,0:T(8,128)(2,1)} %get-tuple-element.15.fl_in, ...), custom_call_target="tpu_custom_call" | custom-call | tf_op jit(solution)/shard_map/block_solve/pallas_call | solution.py:403
  (21 shorter events, 0.8 us)
Async XLA Ops:
  0.6 1.5 copy-start
  2.4 12.6 %collective-permute-start.2 = (f32[448,128]{1,0:T(8,128)S(1)}, f32[448,128]{1,0:T(8,128)S(1)}, u32[]{:S(2)}, u32[]{:S(2)}) collective-permute-start(f32[448,128]{1,0:T(8,128)S(1)} %get-tuple-element.22), channel_id=1, source_target_pairs={{0,192},{32,224},{64,0},{96,32},{128,64},{160,96},{192,128},{224,1... | collective-permute-start | bytes 688136 | tf_op jit(solution)/shard_map/ppermute | solution.py:328
  5.8 9.2 %collective-permute-start.1 = (f32[448,128]{1,0:T(8,128)S(1)}, f32[448,128]{1,0:T(8,128)S(1)}, u32[]{:S(2)}, u32[]{:S(2)}) collective-permute-start(f32[448,128]{1,0:T(8,128)S(1)} %get-tuple-element.22), channel_id=1, source_target_pairs={{0,128},{32,160},{64,192},{96,224},{128,0},{160,32},{192,64},{224,... | collective-permute-start | bytes 688136 | tf_op jit(solution)/shard_map/ppermute | solution.py:328
  6.3 13.4 %collective-permute-start = (f32[448,128]{1,0:T(8,128)S(1)}, f32[448,128]{1,0:T(8,128)S(1)}, u32[]{:S(2)}, u32[]{:S(2)}) collective-permute-start(f32[448,128]{1,0:T(8,128)S(1)} %get-tuple-element.22), channel_id=1, source_target_pairs={{0,64},{32,96},{64,128},{96,160},{128,192},{160,224},{192,0},{224,... | collective-permute-start | bytes 688136 | tf_op jit(solution)/shard_map/ppermute | solution.py:328
  19.8 2.7 %copy-start.2 = (f32[4,448,128]{2,1,0:T(8,128)}, f32[4,448,128]{2,1,0:T(8,128)S(1)}, u32[]{:S(2)}) copy-start(f32[4,448,128]{2,1,0:T(8,128)S(1)} %pad_maximum_fusion.1.mine) | copy-start | bytes 2752516
  19.8 2.7 %collective-permute-start.3 = (f32[4,448,128]{2,1,0:T(8,128)S(1)}, f32[4,448,128]{2,1,0:T(8,128)S(1)}, u32[]{:S(2)}, u32[]{:S(2)}) collective-permute-start(f32[4,448,128]{2,1,0:T(8,128)S(1)} %pad_maximum_fusion.1.mine), channel_id=1, source_target_pairs={{0,32},{32,0},{64,96},{96,64},{128,160},{160,128},{192,224},{224,1... | collective-permute-start | bytes 2752520 | tf_op jit(solution)/shard_map/ppermute | solution.py:353
  22.5 1.0 copy-start.3
  37.9 3.8 %collective-permute-start.4 = (f32[2912,128]{1,0:T(8,128)}, f32[2912,128]{1,0:T(8,128)S(1)}, u32[]{:S(2)}, u32[]{:S(2)}) collective-permute-start(f32[2912,128]{1,0:T(8,128)} %get-tuple-element.13), channel_id=1, source_target_pairs={{0,32},{32,0},{64,96},{96,64},{128,160},{160,128},{192,224},{224,1... | collective-permute-start | bytes 4472840 | tf_op jit(solution)/shard_map/ppermute | solution.py:382
  44.0 11.6 %collective-permute-start.7 = (f32[728,128]{1,0:T(8,128)}, f32[728,128]{1,0:T(8,128)}, u32[]{:S(2)}, u32[]{:S(2)}) collective-permute-start(f32[728,128]{1,0:T(8,128)} %get-tuple-element.17), channel_id=1, source_target_pairs={{0,192},{32,56},{1,193},{33,57},{2,194},{34,58},{3,195},{35,59},{4... | collective-permute-start | bytes 1118216 | tf_op jit(solution)/shard_map/ppermute | solution.py:328
  46.7 8.8 %collective-permute-start.6 = (f32[728,128]{1,0:T(8,128)}, f32[728,128]{1,0:T(8,128)}, u32[]{:S(2)}, u32[]{:S(2)}) collective-permute-start(f32[728,128]{1,0:T(8,128)} %get-tuple-element.18), channel_id=1, source_target_pairs={{0,128},{32,48},{1,129},{33,49},{2,130},{34,50},{3,131},{35,51},{4... | collective-permute-start | bytes 1118216 | tf_op jit(solution)/shard_map/ppermute | solution.py:328
  47.0 11.9 %collective-permute-start.5 = (f32[728,128]{1,0:T(8,128)}, f32[728,128]{1,0:T(8,128)}, u32[]{:S(2)}, u32[]{:S(2)}) collective-permute-start(f32[728,128]{1,0:T(8,128)} %get-tuple-element.16), channel_id=1, source_target_pairs={{0,64},{32,40},{1,65},{33,41},{2,66},{34,42},{3,67},{35,43},{4,68}... | collective-permute-start | bytes 1118216 | tf_op jit(solution)/shard_map/ppermute | solution.py:328
  101.1 6.8 %collective-permute-start.10 = (f32[728,128]{1,0:T(8,128)S(1)}, f32[728,128]{1,0:T(8,128)S(1)}, u32[]{:S(2)}, u32[]{:S(2)}) collective-permute-start(f32[728,128]{1,0:T(8,128)S(1)} %get-tuple-element.20), channel_id=1, source_target_pairs={{0,192},{32,56},{1,193},{33,57},{2,194},{34,58},{3,195},{35,59},{4... | collective-permute-start | bytes 1118216 | tf_op jit(solution)/shard_map/ppermute | solution.py:328
  101.2 8.1 %collective-permute-start.9 = (f32[728,128]{1,0:T(8,128)S(1)}, f32[728,128]{1,0:T(8,128)S(1)}, u32[]{:S(2)}, u32[]{:S(2)}) collective-permute-start(f32[728,128]{1,0:T(8,128)S(1)} %get-tuple-element.20), channel_id=1, source_target_pairs={{0,128},{32,48},{1,129},{33,49},{2,130},{34,50},{3,131},{35,51},{4... | collective-permute-start | bytes 1118216 | tf_op jit(solution)/shard_map/ppermute | solution.py:328
  101.3 12.2 %collective-permute-start.8 = (f32[728,128]{1,0:T(8,128)S(1)}, f32[728,128]{1,0:T(8,128)S(1)}, u32[]{:S(2)}, u32[]{:S(2)}) collective-permute-start(f32[728,128]{1,0:T(8,128)S(1)} %get-tuple-element.20), channel_id=1, source_target_pairs={{0,64},{32,40},{1,65},{33,41},{2,66},{34,42},{3,67},{35,43},{4,68}... | collective-permute-start | bytes 1118216 | tf_op jit(solution)/shard_map/ppermute | solution.py:328
  113.6 8.3 %copy-start.1 = (f32[4,728,128]{2,1,0:T(8,128)}, f32[4,728,128]{2,1,0:T(8,128)S(1)}, u32[]{:S(2)}) copy-start(f32[4,728,128]{2,1,0:T(8,128)S(1)} %pad_maximum_fusion.own) | copy-start | bytes 4472836
  113.6 8.3 %collective-permute-start.11 = (f32[4,728,128]{2,1,0:T(8,128)S(1)}, f32[4,728,128]{2,1,0:T(8,128)}, u32[]{:S(2)}, u32[]{:S(2)}) collective-permute-start(f32[4,728,128]{2,1,0:T(8,128)S(1)} %pad_maximum_fusion.own), channel_id=1, source_target_pairs={{0,32},{32,0},{64,96},{96,64},{128,160},{160,128},{192,224},{224,1... | collective-permute-start | bytes 4472840 | tf_op jit(solution)/shard_map/ppermute | solution.py:400
